TPU v7x, 32 devices: a whole 2x2x4 slice. The times are simulated.
32 devices in a mesh: grp: 2 (over y), vec: 4 (over z), occ: 2 (over x), wlk: 2 (over core).
Axes of the slice: x: 2, y: 2, z: 4, core: 2. Of those that a mesh axis runs over, the one named last changes fastest.
Arguments:
- chol_half: bfloat16 [256, 256, 2048], P(('grp', 'vec'), 'occ'), parts along dimension 0, may hold values from -0.046875 to 0.046875
- theta: bfloat16 [8, 2048, 256], P(('grp', 'wlk'), 'vec', 'occ'), parts along dimension 0, may hold values from -6 to 6
Outputs:
- theta_grad: float32 [8, 2048, 256], P(('grp', 'wlk'), 'vec', 'occ'), parts along dimension 0
There are 2 independent parts, one for each index of `grp`. A program takes and returns all parts, laid end to end along the dimension named above; each array names one. Nothing has to cross between parts.
All inputs are finite; a program needn't handle non-finite values.
Results may differ from a plain program's by a relative error of at most 0.0042.
Values may be sent and summed in bfloat16 or wider, within the bound.
No kernel may reach another device: no remote copies, remote signals or barrier semaphores. Data moves between devices by JAX's collectives and lax.ppermute only.
A program may use at most 64 MiB of HBM per device.

v0:
```python
import jax
import jax.numpy as jnp
from jax import lax
from jax.sharding import PartitionSpec as P


def on_device(chol_half, theta):
    widened = lax.all_gather(theta, "occ", axis=2, tiled=True)
    factor_rows = chol_half
    amplitude_sums = jnp.einsum(
        "gip,wpj->wgij",
        factor_rows,
        lax.all_gather(widened, "vec", axis=1, tiled=True),
        preferred_element_type=jnp.float32,
    )
    amplitudes = amplitude_sums.astype(jnp.bfloat16)
    swapped = lax.all_to_all(amplitudes, "occ", split_axis=3, concat_axis=2, tiled=True)
    factor_rows = chol_half
    summed_rows = lax.psum_scatter(
        jnp.einsum("gap,wgba->pwb", factor_rows, swapped, preferred_element_type=jnp.float32),
        "vec",
        scatter_dimension=0,
        tiled=True,
    )
    owned = lax.psum_scatter(summed_rows, "occ", scatter_dimension=2, tiled=True)
    return -jnp.transpose(owned, (1, 0, 2))


def solution(mesh):
    placed = (P(("grp", "vec"), "occ", None), P(("grp", "wlk"), "vec", "occ"))
    return jax.shard_map(
        on_device,
        mesh=mesh,
        in_specs=placed,
        out_specs=P(("grp", "wlk"), "vec", "occ"),
        check_vma=False,
    )
```

profile of v0, /device:TPU:0, one launch (start us, length us, event | category | flops | bytes accessed | tf_op | source)
XLA Modules:
  0.0 259.8 jit_solution(8337746905256795681)
XLA Ops:
  6.5 0.0 all-gather.2.cloned.1.call-start
  6.5 1.1 copy.6
  7.6 10.0 %all_gather.6 = bf16[2,512,256]{1,2,0:T(8,128)(2,1)} all-gather(bf16[2,512,128]{1,2,0:T(8,128)(2,1)S(1)} %copy.6), channel_id=1, replica_groups=mesh['grp'=2,'vec'=4,'occ'=2,'wlk'=2] {'occ'}, dimensions={2}, use_global_device_ids=true | all-gather | bytes 786432 | tf_op jit(solution)/shard_map/all_gather | solution.py:8
  17.7 0.0 all-gather.2.cloned.1.call-update
  17.7 0.0 reduce-scatter.3.cloned.1.call-start
  17.7 47.3 %all-gather.2.cloned.1.call-done = bf16[2,2048,256]{1,2,0:T(8,128)(2,1)} async-done(((bf16[2,512,256]{1,2,0:T(8,128)(2,1)}), bf16[2,2048,256]{1,2,0:T(8,128)(2,1)}) %all-gather.2.cloned.1.call-update) | async-done | bytes 2097168 | tf_op jit(solution)/shard_map/all_gather | solution.py:13
  65.0 12.4 %convert_bitcast_fusion = bf16[2,32,128,256]{2,3,1,0:T(8,128)(2,1)S(1)} fusion(bf16[32,128,2048]{2,1,0:T(8,128)(2,1)} %param.2, bf16[2,2048,256]{1,2,0:T(8,128)(2,1)} %all-gather.2.cloned.1.call-done), kind=kOutput, calls=%fused_computation.4 | convolution fusion | flops 8592031744 | bytes 23068672 | tf_op jit(solution)/shard_map/gip,wpj->wgij/dot_general | solution.py:10
  77.4 2.7 %copy.7 = bf16[2,32,128,256]{2,1,0,3:T(8,128)(2,1)S(1)} copy(bf16[2,32,128,256]{2,3,1,0:T(8,128)(2,1)S(1)} %convert_bitcast_fusion) | data formatting | bytes 8388608 | tf_op jit(solution)/shard_map/convert_element_type | solution.py:16
  80.1 51.1 %all_to_all.18 = bf16[2,32,128,256]{2,1,0,3:T(8,128)(2,1)} all-to-all(bf16[2,32,128,256]{2,1,0,3:T(8,128)(2,1)S(1)} %copy.7), channel_id=1, replica_groups=mesh['grp'=2,'vec'=4,'occ'=2,'wlk'=2] {'occ'}, dimensions={3} | all-to-all | bytes 8388608 | tf_op jit(solution)/shard_map/all_to_all | solution.py:17
  131.3 7.5 %copy.8 = bf16[2,32,128,2,128]{4,2,3,1,0:T(8,128)(2,1)} copy(bf16[2,32,128,2,128]{2,1,0,4,3:T(8,128)(2,1)} %bitcast.28) | data formatting | bytes 8388608 | tf_op jit(solution)/shard_map/all_to_all | solution.py:17
  138.8 14.1 %fusion.4 = f32[2048,2,256]{0,2,1:T(8,128)} fusion(bf16[2,32,256,128]{3,2,1,0:T(8,128)(2,1)} %bitcast.29, bf16[32,128,2048]{2,1,0:T(8,128)(2,1)} %param.2), kind=kOutput, calls=%fused_computation.5 | convolution fusion | flops 8589934592 | bytes 25165824 | tf_op jit(solution)/shard_map/gap,wgba->pwb/dot_general | solution.py:20
  152.9 0.0 reduce-scatter.3.cloned.1.call-update
  152.9 0.0 reduce-scatter.5.cloned.1.call-start
  153.0 75.0 %reduce-scatter.3.cloned.1.call-done = f32[512,2,256]{0,2,1:T(8,128)} async-done(((f32[2048,2,256]{0,2,1:T(8,128)}), f32[512,2,256]{0,2,1:T(8,128)}) %reduce-scatter.3.cloned.1.call-update) | async-done | bytes 1048592 | tf_op jit(solution)/shard_map/reduce_scatter | solution.py:19
  228.0 0.0 reduce-scatter.5.cloned.1.call-update
  228.0 23.1 %reduce-scatter.5.cloned.1.call-done = f32[512,2,128]{0,2,1:T(8,128)} async-done(((f32[512,2,256]{0,2,1:T(8,128)}), f32[512,2,128]{0,2,1:T(8,128)}) %reduce-scatter.5.cloned.1.call-update) | async-done | bytes 524304 | tf_op jit(solution)/shard_map/reduce_scatter | solution.py:25
  251.2 1.1 negate_bitcast_fusion
  252.3 1.0 copy.9
Async XLA Ops:
  6.5 58.5 %all-gather.2.cloned.1.call-start = ((), (), s32[]{:S(2)}) async-start(), calls=%async_computation.3 | async-start | bytes 2621440 | tf_op jit(solution)/shard_map/all_gather | solution.py:13
  17.7 210.3 %reduce-scatter.3.cloned.1.call-start = ((), (), s32[]{:S(2)}) async-start(), calls=%async_computation.4 | async-start | bytes 5242880 | tf_op jit(solution)/shard_map/reduce_scatter | solution.py:19
  152.9 98.2 %reduce-scatter.5.cloned.1.call-start = ((), (), s32[]{:S(2)}) async-start(), calls=%async_computation.5 | async-start | bytes 1572864 | tf_op jit(solution)/shard_map/reduce_scatter | solution.py:25
Sparse Core Ops, SparseCore 0:
  17.8 47.1 all-gather.1
  153.0 74.9 reduce-scatter.2
  230.2 20.8 reduce-scatter.4
where the time goes:
time: 260 us
  waiting for transfers between devices  145 us (56%)
  blocking collectives  61.2 us (24%)
  matrix products  26.5 us (10%)
  between operations  13.1 us (5%)
  local copies, waits for them, and re-layouts  12.3 us (5%)
    reduce_scatter x1, waiting for transfers between devices, on_device(): lax.psum_scatter(jnp.einsum('gap,wgba->pwb', factor_rows, swapped, prefer...  75 us
    all_to_all x1, blocking collectives, on_device(): lax.all_to_all(amplitudes, 'occ', split_axis=3, concat_axis=2, tiled=True)  51.1 us
    all_gather x1, waiting for transfers between devices, on_device(): lax.all_gather(widened, 'vec', axis=1, tiled=True)  47.3 us
    reduce_scatter x1, waiting for transfers between devices, on_device(): lax.psum_scatter(summed_rows, 'occ', scatter_dimension=2, tiled=True)  23.1 us
    dot_general x1, matrix products, on_device(): jnp.einsum('gap,wgba->pwb', factor_rows, swapped, preferred_element_type=...  14.1 us
    dot_general x1, matrix products, on_device(): jnp.einsum('gip,wpj->wgij', factor_rows, lax.all_gather(widened, 'vec', a...  12.4 us
    all_gather x1, blocking collectives, on_device(): widened = lax.all_gather(theta, 'occ', axis=2, tiled=True)  10 us
    all_to_all x1, local copies, waits for them, and re-layouts, on_device(): lax.all_to_all(amplitudes, 'occ', split_axis=3, concat_axis=2, tiled=True)  7.48 us
  transfers between devices with their start and end apart: 3, of which 3 were waited for; matrix products, arithmetic and copies ran while one was open for 0% of the time, Pallas kernels for 0%

commit v1 on v0

v1 whole, which is shorter than its diff:
```python
import functools

import jax
import jax.numpy as jnp
from jax import lax
from jax.experimental import pallas as pl
from jax.experimental.pallas import tpu as pltpu
from jax.sharding import PartitionSpec as P


AXES = ("grp", "vec", "occ", "wlk")
HALVES = 2
LOADS = 4
SMALL = pltpu.CompilerParams(vmem_limit_bytes=24 * 2**20)


def general(chol_half, theta):
    widened = lax.all_gather(theta, "occ", axis=2, tiled=True)
    amplitude_sums = jnp.einsum(
        "gip,wpj->wgij",
        chol_half,
        lax.all_gather(widened, "vec", axis=1, tiled=True),
        preferred_element_type=jnp.float32,
    )
    amplitudes = amplitude_sums.astype(jnp.bfloat16)
    swapped = lax.all_to_all(amplitudes, "occ", split_axis=3, concat_axis=2, tiled=True)
    summed_rows = lax.psum_scatter(
        jnp.einsum("gap,wgba->pwb", chol_half, swapped, preferred_element_type=jnp.float32),
        "vec",
        scatter_dimension=0,
        tiled=True,
    )
    owned = lax.psum_scatter(summed_rows, "occ", scatter_dimension=2, tiled=True)
    return -jnp.transpose(owned, (1, 0, 2))


VMEM = pl.BlockSpec(memory_space=pltpu.VMEM)
SMEM = pl.BlockSpec(memory_space=pltpu.SMEM)


def peer(position, hop, shards, back=False):
    if shards & (shards - 1) == 0:
        return position ^ hop
    return (position + (shards - hop if back else hop)) % shards


def load_body(first, source, out, arrived):
    copy = pltpu.make_async_copy(source.at[pl.ds(first, out.shape[0])], out, arrived)
    copy.start()
    copy.wait()


def loaded(factors, first, count):
    return pl.pallas_call(
        functools.partial(load_body, first),
        in_specs=[pl.BlockSpec(memory_space=pl.ANY)],
        out_specs=VMEM,
        out_shape=pltpu.VMEM((count, factors.shape[1]), factors.dtype),
        scratch_shapes=[pltpu.SemaphoreType.DMA],
        compiler_params=SMALL,
    )(factors)


def amplitude_body(shards, loads, half, place, *refs):
    factors, pieces, own, far, rows = refs[:loads], refs[loads:-3], refs[-3], refs[-2], refs[-1]
    owned, width = pieces[0].shape[0], own.shape[1]
    for step in range(shards):
        at = pl.multiple_of(place[step] * owned, owned)
        if len(pieces) == shards:
            rows[pl.ds(at, owned), :] = pieces[step][...]
        else:
            rows[pl.ds(at, owned), :width] = pieces[step][...]
            rows[pl.ds(at, owned), width:] = pieces[shards + step][...]
    part, at = width // HALVES, 0
    for chunk in factors:
        lows = range(half * part, chunk.shape[0], width)
        taken = jnp.concatenate([chunk[low : low + part, :] for low in lows], axis=0)
        sums = jnp.dot(taken, rows[...], preferred_element_type=jnp.float32).astype(jnp.bfloat16)
        own[at : at + sums.shape[0], :] = sums[:, :width]
        far[at : at + sums.shape[0], :] = sums[:, width:]
        at += sums.shape[0]


def amplitudes_of(place, factors, pieces, half, width, shards):
    orbitals = factors[0].shape[1]
    count = sum(chunk.shape[0] for chunk in factors) // HALVES
    return pl.pallas_call(
        functools.partial(amplitude_body, shards, len(factors), half),
        in_specs=[SMEM] + [VMEM] * (len(factors) + len(pieces)),
        out_specs=[VMEM] * 2,
        scratch_shapes=[pltpu.VMEM((orbitals, 2 * width), jnp.bfloat16)],
        out_shape=[jax.ShapeDtypeStruct((count, width), jnp.bfloat16)] * 2,
        compiler_params=SMALL,
        cost_estimate=pl.CostEstimate(flops=4 * count * orbitals * width, transcendentals=0, bytes_accessed=2 * count * orbitals),
    )(place, *factors, *pieces)


def gradient_body(shards, loads, groups, place, own, far, *refs):
    factors, outs, sums = refs[:loads], refs[loads:-1], refs[-1]
    width = own.shape[1]
    part, at = width // HALVES, 0
    for chunk in factors:
        vectors = range(at, at + chunk.shape[0] // width)
        wide = [jnp.concatenate([side[g * part : (g + 1) * part, :] for g in vectors], axis=1) for side in (own, far)]
        grown = jnp.dot(jnp.concatenate(wide, axis=0), chunk[...], preferred_element_type=jnp.float32)
        if at == 0:
            sums[...] = grown
        else:
            sums[...] += grown
        at += len(vectors)
    owned = sums.shape[1] // shards
    for hop in range(shards):
        low = pl.multiple_of(place[shards + hop] * owned, owned)
        if groups is None:
            outs[hop][...] = sums[:, pl.ds(low, owned)].astype(outs[hop].dtype)
            continue
        outs[hop][...] = sums[:part, pl.ds(low, owned)].astype(outs[hop].dtype)
        for group, hops in enumerate(groups):
            if hop in hops:
                to = hops.index(hop) * owned
                outs[shards + group][:, to : to + owned] = sums[part:, pl.ds(low, owned)].astype(jnp.bfloat16)


def gradients_of(place, factors, own, far, shards, groups=None):
    orbitals, width = factors[0].shape[1], own.shape[1]
    part, owned = width // HALVES, orbitals // shards
    rows = part if groups else 2 * part
    outs = [jax.ShapeDtypeStruct((rows, owned), jnp.bfloat16 if hop else jnp.float32) for hop in range(shards)]
    if groups:
        outs = [jax.ShapeDtypeStruct((part, owned), jnp.float32)] * shards
        outs += [jax.ShapeDtypeStruct((part, owned * len(hops)), jnp.bfloat16) for hops in groups]
    count = sum(chunk.shape[0] for chunk in factors)
    return pl.pallas_call(
        functools.partial(gradient_body, shards, len(factors), groups),
        in_specs=[SMEM] + [VMEM] * (2 + len(factors)),
        out_specs=[VMEM] * len(outs),
        scratch_shapes=[pltpu.VMEM((2 * part, orbitals), jnp.float32)],
        out_shape=outs,
        compiler_params=SMALL,
        cost_estimate=pl.CostEstimate(flops=4 * count * orbitals * part, transcendentals=0, bytes_accessed=2 * count * orbitals),
    )(place, own, far, *factors)


def split_body(*refs):
    total = refs[0][...].astype(jnp.float32)
    for part in refs[1:-2]:
        total = total + part[...].astype(jnp.float32)
    half = total.shape[0] // 2
    refs[-2][...] = total[:half]
    refs[-1][...] = total[half:].astype(jnp.bfloat16)


def split_sum(parts):
    rows, columns = parts[0].shape
    outs = [jax.ShapeDtypeStruct((rows // 2, columns), kind) for kind in (jnp.float32, jnp.bfloat16)]
    return pl.pallas_call(split_body, out_shape=outs, compiler_params=SMALL)(*parts)


def join_body(came, *refs):
    count = len(refs) // 2
    for at in range(count):
        own, out = refs[at], refs[count + at]
        columns = own.shape[1]
        out[...] = (own[...] + came[:, at * columns : (at + 1) * columns].astype(jnp.float32)).astype(out.dtype)


def join_sums(came, owns, kinds):
    outs = [jax.ShapeDtypeStruct(own.shape, kind) for own, kind in zip(owns, kinds)]
    return pl.pallas_call(join_body, out_shape=outs, compiler_params=SMALL)(came, *owns)


def total_body(counts, *refs):
    out, at = refs[-1], 0
    for walker, halves in enumerate(counts):
        rows = []
        for count in halves:
            total = refs[at][...].astype(jnp.float32)
            for part in refs[at + 1 : at + count]:
                total = total + part[...].astype(jnp.float32)
            rows.append(total)
            at += count
        out[walker] = -jnp.concatenate(rows, axis=0).T


def totals_of(pieces):
    part, owned = pieces[0][0][0].shape
    return pl.pallas_call(
        functools.partial(total_body, [[len(half) for half in walker] for walker in pieces]),
        out_shape=jax.ShapeDtypeStruct((len(pieces), owned, part * HALVES), jnp.float32),
        compiler_params=SMALL,
    )(*[piece for walker in pieces for half in walker for piece in half])


def paired(shape, chol_half, theta):
    return in_order(shape, chol_half, theta)


def in_order(shape, chol_half, theta):
    shards = shape["vec"]
    vectors, width, orbitals = chol_half.shape
    walkers = theta.shape[0]
    position = lax.axis_index("vec")
    place = jnp.stack([peer(position, hop, shards, True) for hop in range(shards)] + [peer(position, hop, shards) for hop in range(shards)])
    whole = chol_half.reshape(vectors * width, orbitals)
    factors = []
    for load in range(LOADS):
        factors.append(loaded(whole, load * vectors // LOADS * width, vectors // LOADS * width))

    def flat(grp, vec, occ, wlk):
        return ((grp * shape["vec"] + vec) * shape["occ"] + occ) * shape["wlk"] + wlk

    def moved(value, hop, across=False):
        pairs = [
            (flat(grp, vec, occ, wlk), flat(grp, peer(vec, hop, shards), 1 - occ if across else occ, wlk))
            for grp in range(shape["grp"])
            for vec in range(shards)
            for occ in range(shape["occ"])
            for wlk in range(shape["wlk"])
        ]
        return lax.ppermute(value, AXES, pairs)

    hops = range(1, shards)
    near = [theta[0]] + [moved(theta[0], hop) for hop in hops]
    across = moved(theta, 0, True)
    blocks = [near + [across[0]] + [moved(near[hop], 0, True) for hop in hops]]
    for walker in range(1, walkers):
        both = jnp.concatenate([theta[walker], across[walker]], axis=1)
        blocks.append([both] + [moved(both, hop) for hop in hops])

    stages = walkers * HALVES
    half = shards // 2
    groups = [list(range(half)), list(range(half, shards))]
    sides = []
    for stage in range(stages):
        own, far = amplitudes_of(place, factors, blocks[stage // HALVES], stage % HALVES, width, shards)
        sides.append([own, moved(far, 0, True)])

    pieces = [[] for _ in range(walkers)]
    for stage in range(stages):
        got = gradients_of(place, factors, *sides[stage], shards, groups if stage == stages - 1 else None)
        if stage < stages - 1:
            arrived = [got[0]] + [moved(got[hop], hop) for hop in hops]
            own, far = split_sum(arrived)
            pieces[stage // HALVES].append([own, moved(far, 0, True)])
        else:
            came = [moved(got[shards + at], 0, True) for at in range(len(groups))]
            owned = []
            for at, hops_of in enumerate(groups):
                owned += join_sums(came[at], [got[hop] for hop in hops_of], [jnp.bfloat16 if hop else jnp.float32 for hop in hops_of])
            pieces[stage // HALVES].append([owned[0]] + [moved(owned[hop], hop) for hop in hops])
    return totals_of(pieces)


def solution(mesh):
    placed = (P(("grp", "vec"), "occ", None), P(("grp", "wlk"), "vec", "occ"))
    pairs = mesh.shape["occ"] == 2
    return jax.shard_map(
        functools.partial(paired, dict(mesh.shape)) if pairs else general,
        mesh=mesh,
        in_specs=placed,
        out_specs=P(("grp", "wlk"), "vec", "occ"),
        check_vma=False,
    )
```

time: 260 us -> 118 us (0.45)
  waiting for transfers between devices: 145 us -> 22.3 us
  blocking collectives: 61.2 us -> 0 us
  starting transfers between devices: 0.09 us -> 44.9 us
  Pallas kernels: 0 us -> 26.6 us
  matrix products: 26.5 us -> 0 us
  between operations: 13.1 us -> 0.22 us
  local copies, waits for them, and re-layouts: 12.3 us -> 23.6 us
    reduce_scatter x2 -> x0, waiting for transfers between devices: 98.2 us -> none  [the longest x1 75 us: on_device(): lax.psum_scatter(jnp.einsum('gap,wgba->pwb', factor_rows, swapped, prefer...]
    all_to_all x1 -> x0, blocking collectives: 51.1 us -> none  [on_device(): lax.all_to_all(amplitudes, 'occ', split_axis=3, concat_axis=2, tiled=True)]
    all_gather x1 -> x0, waiting for transfers between devices: 47.3 us -> none  [on_device(): lax.all_gather(widened, 'vec', axis=1, tiled=True)]
    ppermute x0 -> x31, starting transfers between devices: none -> 44.9 us  [moved(): return lax.ppermute(value, AXES, pairs)]
    pallas_call x0 -> x18, Pallas kernels: none -> 26.6 us  [the longest x4 12.3 us: gradients_of(): pl.pallas_call(functools.partial(gradient_body, shards, len(factors), gro...]
    dot_general x2 -> x0, matrix products: 26.5 us -> none  [the longest x1 14.1 us: on_device(): jnp.einsum('gap,wgba->pwb', factor_rows, swapped, preferred_element_type=...]
    ppermute x0 -> x31, waiting for transfers between devices: none -> 22.3 us  [moved(): return lax.ppermute(value, AXES, pairs)]
    unnamed x1 -> x18, local copies, waits for them, and re-layouts: 1.08 us -> 22.5 us
  transfers between devices with their start and end apart: 3 -> 31, of which waited for: 3 -> 8; matrix products, arithmetic and copies ran while one was open for 0% -> 1% of each run, Pallas kernels for 0% -> 22%
where the time goes in v1:
time: 118 us
  starting transfers between devices  44.9 us (38%)
  Pallas kernels  26.6 us (23%)
  local copies, waits for them, and re-layouts  23.6 us (20%)
  waiting for transfers between devices  22.3 us (19%)
    ppermute x31, starting transfers between devices, moved(): return lax.ppermute(value, AXES, pairs)  44.9 us
    unnamed x18, local copies, waits for them, and re-layouts  22.5 us
    ppermute x31, waiting for transfers between devices, moved(): return lax.ppermute(value, AXES, pairs)  22.3 us
    pallas_call x4, Pallas kernels, gradients_of(): pl.pallas_call(functools.partial(gradient_body, shards, len(factors), gro...  12.3 us
    pallas_call x4, Pallas kernels, amplitudes_of(): pl.pallas_call(functools.partial(amplitude_body, shards, len(factors), ha...  12 us
  transfers between devices with their start and end apart: 31, of which 8 were waited for; matrix products, arithmetic and copies ran while one was open for 1% of the time, Pallas kernels for 22%

profile of v1, /device:TPU:0, one launch (start us, length us, event | category | flops | bytes accessed | tf_op | source)
XLA Modules:
  0.0 117.7 jit_solution(14727534728371979540)
XLA Ops:
  0.0 3.0 %collective-permute-start.3 = (bf16[2,512,128]{2,1,0:T(8,128)(2,1)}, bf16[2,512,128]{2,1,0:T(8,128)(2,1)S(1)}, u32[]{:S(2)}, u32[]{:S(2)}) collective-permute-start(bf16[2,512,128]{2,1,0:T(8,128)(2,1)} %param.3), channel_id=1, source_target_pairs={{0,2},{1,3},{2,0},{3,1},{4,6},{5,7},{6,4},{7,5},{8,10},{9,11},{10,... | collective-permute-start | bytes 786440 | tf_op jit(solution)/shard_map/ppermute | solution.py:220
  5.6 2.6 %collective-permute-start.1 = (bf16[512,128]{1,0:T(8,128)(2,1)S(1)}, bf16[512,128]{1,0:T(8,128)(2,1)S(1)}, u32[]{:S(2)}, u32[]{:S(2)}) collective-permute-start(bf16[512,128]{1,0:T(8,128)(2,1)S(1)} %get-tuple-element.78.refs_4_), channel_id=1, source_target_pairs={{0,8},{1,9},{2,10},{3,11},{4,12},{5,13},{6,14},{7,15},{8,0},{9,1},... | collective-permute-start | bytes 393224 | tf_op jit(solution)/shard_map/ppermute | solution.py:220
  8.4 5.8 %copy-done.8 = bf16[32,128,2048]{2,1,0:T(8,128)(2,1)S(1)} copy-done((bf16[32,128,2048]{2,1,0:T(8,128)(2,1)S(1)}, bf16[32,128,2048]{2,1,0:T(8,128)(2,1)}, u32[]{:S(2)}) %copy-start.8) | copy-done | bytes 16777240
  14.5 2.0 %copy-done = bf16[1024,2048]{1,0:T(8,128)(2,1)} copy-done((bf16[1024,2048]{1,0:T(8,128)(2,1)}, bf16[1024,2048]{1,0:T(8,128)(2,1)S(1)}, u32[]{:S(2)}) %copy-start) | copy-done | bytes 4194328
  16.8 2.0 %copy-done.2 = bf16[1024,2048]{1,0:T(8,128)(2,1)} copy-done((bf16[1024,2048]{1,0:T(8,128)(2,1)}, bf16[1024,2048]{1,0:T(8,128)(2,1)S(1)}, u32[]{:S(2)}) %copy-start.2) | copy-done | bytes 4194328
  19.1 2.1 %copy-done.4 = bf16[1024,2048]{1,0:T(8,128)(2,1)} copy-done((bf16[1024,2048]{1,0:T(8,128)(2,1)}, bf16[1024,2048]{1,0:T(8,128)(2,1)S(1)}, u32[]{:S(2)}) %copy-start.4) | copy-done | bytes 4194328
  21.5 1.9 %copy-done.6 = bf16[1024,2048]{1,0:T(8,128)(2,1)} copy-done((bf16[1024,2048]{1,0:T(8,128)(2,1)}, bf16[1024,2048]{1,0:T(8,128)(2,1)S(1)}, u32[]{:S(2)}) %copy-start.6) | copy-done | bytes 4194328
  23.9 1.7 %collective-permute-start.5 = (bf16[512,128]{1,0:T(8,128)(2,1)S(1)}, bf16[512,128]{1,0:T(8,128)(2,1)S(1)}, u32[]{:S(2)}, u32[]{:S(2)}) collective-permute-start(bf16[512,128]{1,0:T(8,128)(2,1)S(1)} %collective-permute-done.1.refs_6_), channel_id=1, source_target_pairs={{0,2},{1,3},{2,0},{3,1},{4,6},{5,7},{6,4},{7,5},{8,10},{9,11},{10,... | collective-permute-start | bytes 393224 | tf_op jit(solution)/shard_map/ppermute | solution.py:220
  26.9 3.5 %collective-permute-start.18 = (bf16[512,256]{1,0:T(8,128)(2,1)S(1)}, bf16[512,256]{1,0:T(8,128)(2,1)S(1)}, u32[]{:S(2)}, u32[]{:S(2)}) collective-permute-start(bf16[512,256]{1,0:T(8,128)(2,1)S(1)} %pad_maximum_fusion.refs_4_), channel_id=1, source_target_pairs={{0,8},{1,9},{2,10},{3,11},{4,12},{5,13},{6,14},{7,15},{8,0},{9,1},... | collective-permute-start | bytes 786440 | tf_op jit(solution)/shard_map/ppermute | solution.py:220
  30.4 3.1 %collective-permute-start.19 = (bf16[512,256]{1,0:T(8,128)(2,1)S(1)}, bf16[512,256]{1,0:T(8,128)(2,1)S(1)}, u32[]{:S(2)}, u32[]{:S(2)}) collective-permute-start(bf16[512,256]{1,0:T(8,128)(2,1)S(1)} %pad_maximum_fusion.refs_4_), channel_id=1, source_target_pairs={{0,12},{1,13},{2,14},{3,15},{4,8},{5,9},{6,10},{7,11},{8,4},{9,5},... | collective-permute-start | bytes 786440 | tf_op jit(solution)/shard_map/ppermute | solution.py:220
  33.5 2.2 %copy-done.1 = bf16[1024,2048]{1,0:T(8,128)(2,1)S(1)} copy-done((bf16[1024,2048]{1,0:T(8,128)(2,1)S(1)}, bf16[1024,2048]{1,0:T(8,128)(2,1)}, u32[]{:S(2)}) %copy-start.1) | copy-done | bytes 4194328
  35.7 2.2 %copy-done.3 = bf16[1024,2048]{1,0:T(8,128)(2,1)S(1)} copy-done((bf16[1024,2048]{1,0:T(8,128)(2,1)S(1)}, bf16[1024,2048]{1,0:T(8,128)(2,1)}, u32[]{:S(2)}) %copy-start.3) | copy-done | bytes 4194328
  37.9 2.2 %copy-done.5 = bf16[1024,2048]{1,0:T(8,128)(2,1)S(1)} copy-done((bf16[1024,2048]{1,0:T(8,128)(2,1)S(1)}, bf16[1024,2048]{1,0:T(8,128)(2,1)}, u32[]{:S(2)}) %copy-start.5) | copy-done | bytes 4194328
  40.1 2.2 %copy-done.7 = bf16[1024,2048]{1,0:T(8,128)(2,1)S(1)} copy-done((bf16[1024,2048]{1,0:T(8,128)(2,1)S(1)}, bf16[1024,2048]{1,0:T(8,128)(2,1)}, u32[]{:S(2)}) %copy-start.7) | copy-done | bytes 4194328
  42.3 3.1 %shard_map.32 = (bf16[2048,128]{1,0:T(8,128)(2,1)S(1)}, bf16[2048,128]{1,0:T(8,128)(2,1)S(1)}) custom-call(s32[8]{0:T(128)S(1)} %stack.23.place, bf16[1024,2048]{1,0:T(8,128)(2,1)S(1)} %copy-done.1, bf16[1024,2048]{1,0:T(8,128)(2,1)S(1)} %copy-done.3, bf16[1024,2048]{1,0:T(8,128)(2,1)S(1)} %copy-done.5, bf16[1024,2048]{1,0:T(8,128)(2,1)S(1)} %copy-done.7, ...), custom_call_target="tpu_custom_call" | custom-call | flops 2147483648 | bytes 8388608 | tf_op jit(solution)/shard_map/pallas_call | solution.py:87
  45.9 3.1 %shard_map.35 = (bf16[2048,128]{1,0:T(8,128)(2,1)S(1)}, bf16[2048,128]{1,0:T(8,128)(2,1)S(1)}) custom-call(s32[8]{0:T(128)S(1)} %stack.23.place, bf16[1024,2048]{1,0:T(8,128)(2,1)S(1)} %copy-done.1, bf16[1024,2048]{1,0:T(8,128)(2,1)S(1)} %copy-done.3, bf16[1024,2048]{1,0:T(8,128)(2,1)S(1)} %copy-done.5, bf16[1024,2048]{1,0:T(8,128)(2,1)S(1)} %copy-done.7, ...), custom_call_target="tpu_custom_call" | custom-call | flops 2147483648 | bytes 8388608 | tf_op jit(solution)/shard_map/pallas_call | solution.py:87
  50.6 2.9 %shard_map.38 = (bf16[2048,128]{1,0:T(8,128)(2,1)S(1)}, bf16[2048,128]{1,0:T(8,128)(2,1)S(1)}) custom-call(s32[8]{0:T(128)S(1)} %stack.23.place, bf16[1024,2048]{1,0:T(8,128)(2,1)S(1)} %copy-done.1, bf16[1024,2048]{1,0:T(8,128)(2,1)S(1)} %copy-done.3, bf16[1024,2048]{1,0:T(8,128)(2,1)S(1)} %copy-done.5, bf16[1024,2048]{1,0:T(8,128)(2,1)S(1)} %copy-done.7, ...), custom_call_target="tpu_custom_call" | custom-call | flops 2147483648 | bytes 8388608 | tf_op jit(solution)/shard_map/pallas_call | solution.py:87
  54.1 2.9 %shard_map.41 = (bf16[2048,128]{1,0:T(8,128)(2,1)S(1)}, bf16[2048,128]{1,0:T(8,128)(2,1)S(1)}) custom-call(s32[8]{0:T(128)S(1)} %stack.23.place, bf16[1024,2048]{1,0:T(8,128)(2,1)S(1)} %copy-done.1, bf16[1024,2048]{1,0:T(8,128)(2,1)S(1)} %copy-done.3, bf16[1024,2048]{1,0:T(8,128)(2,1)S(1)} %copy-done.5, bf16[1024,2048]{1,0:T(8,128)(2,1)S(1)} %copy-done.7, ...), custom_call_target="tpu_custom_call" | custom-call | flops 2147483648 | bytes 8388608 | tf_op jit(solution)/shard_map/pallas_call | solution.py:87
  60.2 3.0 %shard_map.33 = (f32[128,512]{1,0:T(8,128)S(1)}, bf16[128,512]{1,0:T(8,128)(2,1)S(1)}, bf16[128,512]{1,0:T(8,128)(2,1)S(1)}, bf16[128,512]{1,0:T(8,128)(2,1)S(1)}) custom-call(s32[8]{0:T(128)S(1)} %stack.23.place, bf16[2048,128]{1,0:T(8,128)(2,1)S(1)} %get-tuple-element.41.own, bf16[2048,128]{1,0:T(8,128)(2,1)S(1)} %collective-permute-done.7.far, ...), custom_call_target="tpu_custom_call" | custom-call | flops 2147483648 | bytes 16777216 | tf_op jit(solution)/shard_map/pallas_call | solution.py:133
  63.7 3.5 %collective-permute-start.9 = (bf16[128,512]{1,0:T(8,128)(2,1)S(1)}, bf16[128,512]{1,0:T(8,128)(2,1)S(1)}, u32[]{:S(2)}, u32[]{:S(2)}) collective-permute-start(bf16[128,512]{1,0:T(8,128)(2,1)S(1)} %get-tuple-element.45), channel_id=1, source_target_pairs={{0,8},{1,9},{2,10},{3,11},{4,12},{5,13},{6,14},{7,15},{8,0},{9,1},... | collective-permute-start | bytes 393224 | tf_op jit(solution)/shard_map/ppermute | solution.py:220
  67.2 4.2 %collective-permute-done.12.far = bf16[2048,128]{1,0:T(8,128)(2,1)S(1)} collective-permute-done((bf16[2048,128]{1,0:T(8,128)(2,1)S(1)}, bf16[2048,128]{1,0:T(8,128)(2,1)S(1)}, u32[]{:S(2)}, u32[]{:S(2)}) %collective-permute-start.12) | collective-permute-done | bytes 524320 | tf_op jit(solution)/shard_map/ppermute | solution.py:220
  71.4 3.4 %collective-permute-start.10 = (bf16[128,512]{1,0:T(8,128)(2,1)S(1)}, bf16[128,512]{1,0:T(8,128)(2,1)S(1)}, u32[]{:S(2)}, u32[]{:S(2)}) collective-permute-start(bf16[128,512]{1,0:T(8,128)(2,1)S(1)} %get-tuple-element.46), channel_id=1, source_target_pairs={{0,12},{1,13},{2,14},{3,15},{4,8},{5,9},{6,10},{7,11},{8,4},{9,5},... | collective-permute-start | bytes 393224 | tf_op jit(solution)/shard_map/ppermute | solution.py:220
  74.8 3.2 %shard_map.36 = (f32[128,512]{1,0:T(8,128)S(1)}, bf16[128,512]{1,0:T(8,128)(2,1)S(1)}, bf16[128,512]{1,0:T(8,128)(2,1)S(1)}, bf16[128,512]{1,0:T(8,128)(2,1)S(1)}) custom-call(s32[8]{0:T(128)S(1)} %stack.23.place, bf16[2048,128]{1,0:T(8,128)(2,1)S(1)} %get-tuple-element.49.own, bf16[2048,128]{1,0:T(8,128)(2,1)S(1)} %collective-permute-done.12.far, ...), custom_call_target="tpu_custom_call" | custom-call | flops 2147483648 | bytes 16777216 | tf_op jit(solution)/shard_map/pallas_call | solution.py:133
  78.0 4.7 %collective-permute-done.20.far = bf16[2048,128]{1,0:T(8,128)(2,1)S(1)} collective-permute-done((bf16[2048,128]{1,0:T(8,128)(2,1)S(1)}, bf16[2048,128]{1,0:T(8,128)(2,1)S(1)}, u32[]{:S(2)}, u32[]{:S(2)}) %collective-permute-start.20) | collective-permute-done | bytes 524320 | tf_op jit(solution)/shard_map/ppermute | solution.py:220
  83.1 3.0 %shard_map.39 = (f32[128,512]{1,0:T(8,128)S(1)}, bf16[128,512]{1,0:T(8,128)(2,1)S(1)}, bf16[128,512]{1,0:T(8,128)(2,1)S(1)}, bf16[128,512]{1,0:T(8,128)(2,1)S(1)}) custom-call(s32[8]{0:T(128)S(1)} %stack.23.place, bf16[2048,128]{1,0:T(8,128)(2,1)S(1)} %get-tuple-element.57.own, bf16[2048,128]{1,0:T(8,128)(2,1)S(1)} %collective-permute-done.20.far, ...), custom_call_target="tpu_custom_call" | custom-call | flops 2147483648 | bytes 16777216 | tf_op jit(solution)/shard_map/pallas_call | solution.py:133
  86.1 3.6 %collective-permute-start.14 = (bf16[128,512]{1,0:T(8,128)(2,1)S(1)}, bf16[128,512]{1,0:T(8,128)(2,1)S(1)}, u32[]{:S(2)}, u32[]{:S(2)}) collective-permute-start(bf16[128,512]{1,0:T(8,128)(2,1)S(1)} %get-tuple-element.53), channel_id=1, source_target_pairs={{0,8},{1,9},{2,10},{3,11},{4,12},{5,13},{6,14},{7,15},{8,0},{9,1},... | collective-permute-start | bytes 393224 | tf_op jit(solution)/shard_map/ppermute | solution.py:220
  90.3 2.4 %collective-permute-done.13.refs_1_ = bf16[128,512]{1,0:T(8,128)(2,1)S(1)} collective-permute-done((bf16[128,512]{1,0:T(8,128)(2,1)S(1)}, bf16[128,512]{1,0:T(8,128)(2,1)S(1)}, u32[]{:S(2)}, u32[]{:S(2)}) %collective-permute-start.13) | collective-permute-done | bytes 131104 | tf_op jit(solution)/shard_map/ppermute | solution.py:220
  94.7 3.0 %shard_map.42 = (f32[64,512]{1,0:T(8,128)S(1)}, f32[64,512]{1,0:T(8,128)S(1)}, f32[64,512]{1,0:T(8,128)S(1)}, f32[64,512]{1,0:T(8,128)S(1)}, bf16[64,1024]{1,0:T(8,128)(2,1)S(1)}, /*index=5*/bf16[64,1024]{1,0:T(8,128)(2,1)S(1)}) custom-call(s32[8]{0:T(128)S(1)} %stack.23.place, bf16[2048,128]{1,0:T(8,128)(2,1)S(1)} %get-tuple-element.65.own, ...), custom_call_target="tpu_custom_call" | custom-call | flops 2147483648 | bytes 16777216 | tf_op jit(solution)/shard_map/pallas_call | solution.py:133
  97.7 4.7 %collective-permute-done.14.refs_2_ = bf16[128,512]{1,0:T(8,128)(2,1)S(1)} collective-permute-done((bf16[128,512]{1,0:T(8,128)(2,1)S(1)}, bf16[128,512]{1,0:T(8,128)(2,1)S(1)}, u32[]{:S(2)}, u32[]{:S(2)}) %collective-permute-start.14) | collective-permute-done | bytes 131104 | tf_op jit(solution)/shard_map/ppermute | solution.py:220
  108.9 1.7 %collective-permute-start.29 = (bf16[64,512]{1,0:T(8,128)(2,1)S(1)}, bf16[64,512]{1,0:T(8,128)(2,1)S(1)}, u32[]{:S(2)}, u32[]{:S(2)}) collective-permute-start(bf16[64,512]{1,0:T(8,128)(2,1)S(1)} %get-tuple-element.75), channel_id=1, source_target_pairs={{0,8},{1,9},{2,10},{3,11},{4,12},{5,13},{6,14},{7,15},{8,0},{9,1},... | collective-permute-start | bytes 196616 | tf_op jit(solution)/shard_map/ppermute | solution.py:220
  112.1 2.8 %collective-permute-done.29.refs_8_ = bf16[64,512]{1,0:T(8,128)(2,1)S(1)} collective-permute-done((bf16[64,512]{1,0:T(8,128)(2,1)S(1)}, bf16[64,512]{1,0:T(8,128)(2,1)S(1)}, u32[]{:S(2)}, u32[]{:S(2)}) %collective-permute-start.29) | collective-permute-done | bytes 65568 | tf_op jit(solution)/shard_map/ppermute | solution.py:220
  114.9 1.8 %collective-permute-done.30.refs_9_ = bf16[64,512]{1,0:T(8,128)(2,1)S(1)} collective-permute-done((bf16[64,512]{1,0:T(8,128)(2,1)S(1)}, bf16[64,512]{1,0:T(8,128)(2,1)S(1)}, u32[]{:S(2)}, u32[]{:S(2)}) %collective-permute-start.30) | collective-permute-done | bytes 65568 | tf_op jit(solution)/shard_map/ppermute | solution.py:220
  (70 shorter events, 24.2 us)
Async XLA Ops:
  0.0 25.9 %collective-permute-start.3 = (bf16[2,512,128]{2,1,0:T(8,128)(2,1)}, bf16[2,512,128]{2,1,0:T(8,128)(2,1)S(1)}, u32[]{:S(2)}, u32[]{:S(2)}) collective-permute-start(bf16[2,512,128]{2,1,0:T(8,128)(2,1)} %param.3), channel_id=1, source_target_pairs={{0,2},{1,3},{2,0},{3,1},{4,6},{5,7},{6,4},{7,5},{8,10},{9,11},{10,... | collective-permute-start | bytes 786440 | tf_op jit(solution)/shard_map/ppermute | solution.py:220
  4.0 19.5 %collective-permute-start = (bf16[512,128]{1,0:T(8,128)(2,1)S(1)}, bf16[512,128]{1,0:T(8,128)(2,1)S(1)}, u32[]{:S(2)}, u32[]{:S(2)}) collective-permute-start(bf16[512,128]{1,0:T(8,128)(2,1)S(1)} %get-tuple-element.78.refs_4_), channel_id=1, source_target_pairs={{0,4},{1,5},{2,6},{3,7},{4,0},{5,1},{6,2},{7,3},{8,12},{9,13},{10,... | collective-permute-start | bytes 393224 | tf_op jit(solution)/shard_map/ppermute | solution.py:220
  5.6 18.2 %collective-permute-start.1 = (bf16[512,128]{1,0:T(8,128)(2,1)S(1)}, bf16[512,128]{1,0:T(8,128)(2,1)S(1)}, u32[]{:S(2)}, u32[]{:S(2)}) collective-permute-start(bf16[512,128]{1,0:T(8,128)(2,1)S(1)} %get-tuple-element.78.refs_4_), channel_id=1, source_target_pairs={{0,8},{1,9},{2,10},{3,11},{4,12},{5,13},{6,14},{7,15},{8,0},{9,1},... | collective-permute-start | bytes 393224 | tf_op jit(solution)/shard_map/ppermute | solution.py:220
  8.2 17.4 %collective-permute-start.2 = (bf16[512,128]{1,0:T(8,128)(2,1)S(1)}, bf16[512,128]{1,0:T(8,128)(2,1)S(1)}, u32[]{:S(2)}, u32[]{:S(2)}) collective-permute-start(bf16[512,128]{1,0:T(8,128)(2,1)S(1)} %get-tuple-element.78.refs_4_), channel_id=1, source_target_pairs={{0,12},{1,13},{2,14},{3,15},{4,8},{5,9},{6,10},{7,11},{8,4},{9,5},... | collective-permute-start | bytes 393224 | tf_op jit(solution)/shard_map/ppermute | solution.py:220
  8.4 5.8 %copy-start.8 = (bf16[32,128,2048]{2,1,0:T(8,128)(2,1)S(1)}, bf16[32,128,2048]{2,1,0:T(8,128)(2,1)}, u32[]{:S(2)}) copy-start(bf16[32,128,2048]{2,1,0:T(8,128)(2,1)} %param.2) | copy-start | bytes 50331652
  23.5 6.9 %collective-permute-start.4 = (bf16[512,128]{1,0:T(8,128)(2,1)S(1)}, bf16[512,128]{1,0:T(8,128)(2,1)S(1)}, u32[]{:S(2)}, u32[]{:S(2)}) collective-permute-start(bf16[512,128]{1,0:T(8,128)(2,1)S(1)} %collective-permute-done.refs_5_), channel_id=1, source_target_pairs={{0,2},{1,3},{2,0},{3,1},{4,6},{5,7},{6,4},{7,5},{8,10},{9,11},{10,... | collective-permute-start | bytes 393224 | tf_op jit(solution)/shard_map/ppermute | solution.py:220
  23.9 9.7 %collective-permute-start.5 = (bf16[512,128]{1,0:T(8,128)(2,1)S(1)}, bf16[512,128]{1,0:T(8,128)(2,1)S(1)}, u32[]{:S(2)}, u32[]{:S(2)}) collective-permute-start(bf16[512,128]{1,0:T(8,128)(2,1)S(1)} %collective-permute-done.1.refs_6_), channel_id=1, source_target_pairs={{0,2},{1,3},{2,0},{3,1},{4,6},{5,7},{6,4},{7,5},{8,10},{9,11},{10,... | collective-permute-start | bytes 393224 | tf_op jit(solution)/shard_map/ppermute | solution.py:220
  25.6 7.9 %collective-permute-start.6 = (bf16[512,128]{1,0:T(8,128)(2,1)S(1)}, bf16[512,128]{1,0:T(8,128)(2,1)S(1)}, u32[]{:S(2)}, u32[]{:S(2)}) collective-permute-start(bf16[512,128]{1,0:T(8,128)(2,1)S(1)} %collective-permute-done.2.refs_7_), channel_id=1, source_target_pairs={{0,2},{1,3},{2,0},{3,1},{4,6},{5,7},{6,4},{7,5},{8,10},{9,11},{10,... | collective-permute-start | bytes 393224 | tf_op jit(solution)/shard_map/ppermute | solution.py:220
  26.0 24.6 %collective-permute-start.17 = (bf16[512,256]{1,0:T(8,128)(2,1)S(1)}, bf16[512,256]{1,0:T(8,128)(2,1)S(1)}, u32[]{:S(2)}, u32[]{:S(2)}) collective-permute-start(bf16[512,256]{1,0:T(8,128)(2,1)S(1)} %pad_maximum_fusion.refs_4_), channel_id=1, source_target_pairs={{0,4},{1,5},{2,6},{3,7},{4,0},{5,1},{6,2},{7,3},{8,12},{9,13},{10,... | collective-permute-start | bytes 786440 | tf_op jit(solution)/shard_map/ppermute | solution.py:220
  26.9 23.6 %collective-permute-start.18 = (bf16[512,256]{1,0:T(8,128)(2,1)S(1)}, bf16[512,256]{1,0:T(8,128)(2,1)S(1)}, u32[]{:S(2)}, u32[]{:S(2)}) collective-permute-start(bf16[512,256]{1,0:T(8,128)(2,1)S(1)} %pad_maximum_fusion.refs_4_), channel_id=1, source_target_pairs={{0,8},{1,9},{2,10},{3,11},{4,12},{5,13},{6,14},{7,15},{8,0},{9,1},... | collective-permute-start | bytes 786440 | tf_op jit(solution)/shard_map/ppermute | solution.py:220
  30.4 20.2 %collective-permute-start.19 = (bf16[512,256]{1,0:T(8,128)(2,1)S(1)}, bf16[512,256]{1,0:T(8,128)(2,1)S(1)}, u32[]{:S(2)}, u32[]{:S(2)}) collective-permute-start(bf16[512,256]{1,0:T(8,128)(2,1)S(1)} %pad_maximum_fusion.refs_4_), channel_id=1, source_target_pairs={{0,12},{1,13},{2,14},{3,15},{4,8},{5,9},{6,10},{7,11},{8,4},{9,5},... | collective-permute-start | bytes 786440 | tf_op jit(solution)/shard_map/ppermute | solution.py:220
  45.3 14.9 %collective-permute-start.7 = (bf16[2048,128]{1,0:T(8,128)(2,1)S(1)}, bf16[2048,128]{1,0:T(8,128)(2,1)S(1)}, u32[]{:S(2)}, u32[]{:S(2)}) collective-permute-start(bf16[2048,128]{1,0:T(8,128)(2,1)S(1)} %get-tuple-element.42), channel_id=1, source_target_pairs={{0,2},{1,3},{2,0},{3,1},{4,6},{5,7},{6,4},{7,5},{8,10},{9,11},{10,... | collective-permute-start | bytes 1572872 | tf_op jit(solution)/shard_map/ppermute | solution.py:220
  49.0 22.4 %collective-permute-start.12 = (bf16[2048,128]{1,0:T(8,128)(2,1)S(1)}, bf16[2048,128]{1,0:T(8,128)(2,1)S(1)}, u32[]{:S(2)}, u32[]{:S(2)}) collective-permute-start(bf16[2048,128]{1,0:T(8,128)(2,1)S(1)} %get-tuple-element.50), channel_id=1, source_target_pairs={{0,2},{1,3},{2,0},{3,1},{4,6},{5,7},{6,4},{7,5},{8,10},{9,11},{10,... | collective-permute-start | bytes 1572872 | tf_op jit(solution)/shard_map/ppermute | solution.py:220
  53.5 29.1 %collective-permute-start.20 = (bf16[2048,128]{1,0:T(8,128)(2,1)S(1)}, bf16[2048,128]{1,0:T(8,128)(2,1)S(1)}, u32[]{:S(2)}, u32[]{:S(2)}) collective-permute-start(bf16[2048,128]{1,0:T(8,128)(2,1)S(1)} %get-tuple-element.58), channel_id=1, source_target_pairs={{0,2},{1,3},{2,0},{3,1},{4,6},{5,7},{6,4},{7,5},{8,10},{9,11},{10,... | collective-permute-start | bytes 1572872 | tf_op jit(solution)/shard_map/ppermute | solution.py:220
  57.1 37.0 %collective-permute-start.25 = (bf16[2048,128]{1,0:T(8,128)(2,1)S(1)}, bf16[2048,128]{1,0:T(8,128)(2,1)S(1)}, u32[]{:S(2)}, u32[]{:S(2)}) collective-permute-start(bf16[2048,128]{1,0:T(8,128)(2,1)S(1)} %get-tuple-element.66), channel_id=1, source_target_pairs={{0,2},{1,3},{2,0},{3,1},{4,6},{5,7},{6,4},{7,5},{8,10},{9,11},{10,... | collective-permute-start | bytes 1572872 | tf_op jit(solution)/shard_map/ppermute | solution.py:220
  63.2 22.9 %collective-permute-start.8 = (bf16[128,512]{1,0:T(8,128)(2,1)S(1)}, bf16[128,512]{1,0:T(8,128)(2,1)S(1)}, u32[]{:S(2)}, u32[]{:S(2)}) collective-permute-start(bf16[128,512]{1,0:T(8,128)(2,1)S(1)} %get-tuple-element.44), channel_id=1, source_target_pairs={{0,4},{1,5},{2,6},{3,7},{4,0},{5,1},{6,2},{7,3},{8,12},{9,13},{10,... | collective-permute-start | bytes 393224 | tf_op jit(solution)/shard_map/ppermute | solution.py:220
  63.7 26.0 %collective-permute-start.9 = (bf16[128,512]{1,0:T(8,128)(2,1)S(1)}, bf16[128,512]{1,0:T(8,128)(2,1)S(1)}, u32[]{:S(2)}, u32[]{:S(2)}) collective-permute-start(bf16[128,512]{1,0:T(8,128)(2,1)S(1)} %get-tuple-element.45), channel_id=1, source_target_pairs={{0,8},{1,9},{2,10},{3,11},{4,12},{5,13},{6,14},{7,15},{8,0},{9,1},... | collective-permute-start | bytes 393224 | tf_op jit(solution)/shard_map/ppermute | solution.py:220
  71.4 18.7 %collective-permute-start.10 = (bf16[128,512]{1,0:T(8,128)(2,1)S(1)}, bf16[128,512]{1,0:T(8,128)(2,1)S(1)}, u32[]{:S(2)}, u32[]{:S(2)}) collective-permute-start(bf16[128,512]{1,0:T(8,128)(2,1)S(1)} %get-tuple-element.46), channel_id=1, source_target_pairs={{0,12},{1,13},{2,14},{3,15},{4,8},{5,9},{6,10},{7,11},{8,4},{9,5},... | collective-permute-start | bytes 393224 | tf_op jit(solution)/shard_map/ppermute | solution.py:220
  82.7 10.1 %collective-permute-start.13 = (bf16[128,512]{1,0:T(8,128)(2,1)S(1)}, bf16[128,512]{1,0:T(8,128)(2,1)S(1)}, u32[]{:S(2)}, u32[]{:S(2)}) collective-permute-start(bf16[128,512]{1,0:T(8,128)(2,1)S(1)} %get-tuple-element.52), channel_id=1, source_target_pairs={{0,4},{1,5},{2,6},{3,7},{4,0},{5,1},{6,2},{7,3},{8,12},{9,13},{10,... | collective-permute-start | bytes 393224 | tf_op jit(solution)/shard_map/ppermute | solution.py:220
  86.1 16.3 %collective-permute-start.14 = (bf16[128,512]{1,0:T(8,128)(2,1)S(1)}, bf16[128,512]{1,0:T(8,128)(2,1)S(1)}, u32[]{:S(2)}, u32[]{:S(2)}) collective-permute-start(bf16[128,512]{1,0:T(8,128)(2,1)S(1)} %get-tuple-element.53), channel_id=1, source_target_pairs={{0,8},{1,9},{2,10},{3,11},{4,12},{5,13},{6,14},{7,15},{8,0},{9,1},... | collective-permute-start | bytes 393224 | tf_op jit(solution)/shard_map/ppermute | solution.py:220
  89.7 13.3 %collective-permute-start.15 = (bf16[128,512]{1,0:T(8,128)(2,1)S(1)}, bf16[128,512]{1,0:T(8,128)(2,1)S(1)}, u32[]{:S(2)}, u32[]{:S(2)}) collective-permute-start(bf16[128,512]{1,0:T(8,128)(2,1)S(1)} %get-tuple-element.54), channel_id=1, source_target_pairs={{0,12},{1,13},{2,14},{3,15},{4,8},{5,9},{6,10},{7,11},{8,4},{9,5},... | collective-permute-start | bytes 393224 | tf_op jit(solution)/shard_map/ppermute | solution.py:220
  90.2 14.3 %collective-permute-start.21 = (bf16[128,512]{1,0:T(8,128)(2,1)S(1)}, bf16[128,512]{1,0:T(8,128)(2,1)S(1)}, u32[]{:S(2)}, u32[]{:S(2)}) collective-permute-start(bf16[128,512]{1,0:T(8,128)(2,1)S(1)} %get-tuple-element.60), channel_id=1, source_target_pairs={{0,4},{1,5},{2,6},{3,7},{4,0},{5,1},{6,2},{7,3},{8,12},{9,13},{10,... | collective-permute-start | bytes 393224 | tf_op jit(solution)/shard_map/ppermute | solution.py:220
  92.8 12.5 %collective-permute-start.22 = (bf16[128,512]{1,0:T(8,128)(2,1)S(1)}, bf16[128,512]{1,0:T(8,128)(2,1)S(1)}, u32[]{:S(2)}, u32[]{:S(2)}) collective-permute-start(bf16[128,512]{1,0:T(8,128)(2,1)S(1)} %get-tuple-element.61), channel_id=1, source_target_pairs={{0,8},{1,9},{2,10},{3,11},{4,12},{5,13},{6,14},{7,15},{8,0},{9,1},... | collective-permute-start | bytes 393224 | tf_op jit(solution)/shard_map/ppermute | solution.py:220
  94.1 12.6 %collective-permute-start.23 = (bf16[128,512]{1,0:T(8,128)(2,1)S(1)}, bf16[128,512]{1,0:T(8,128)(2,1)S(1)}, u32[]{:S(2)}, u32[]{:S(2)}) collective-permute-start(bf16[128,512]{1,0:T(8,128)(2,1)S(1)} %get-tuple-element.62), channel_id=1, source_target_pairs={{0,12},{1,13},{2,14},{3,15},{4,8},{5,9},{6,10},{7,11},{8,4},{9,5},... | collective-permute-start | bytes 393224 | tf_op jit(solution)/shard_map/ppermute | solution.py:220
  102.4 5.1 %collective-permute-start.26 = (bf16[64,1024]{1,0:T(8,128)(2,1)S(1)}, bf16[64,1024]{1,0:T(8,128)(2,1)S(1)}, u32[]{:S(2)}, u32[]{:S(2)}) collective-permute-start(bf16[64,1024]{1,0:T(8,128)(2,1)S(1)} %get-tuple-element.67), channel_id=1, source_target_pairs={{0,2},{1,3},{2,0},{3,1},{4,6},{5,7},{6,4},{7,5},{8,10},{9,11},{10,... | collective-permute-start | bytes 393224 | tf_op jit(solution)/shard_map/ppermute | solution.py:220
  103.0 5.9 %collective-permute-start.28 = (bf16[64,1024]{1,0:T(8,128)(2,1)S(1)}, bf16[64,1024]{1,0:T(8,128)(2,1)S(1)}, u32[]{:S(2)}, u32[]{:S(2)}) collective-permute-start(bf16[64,1024]{1,0:T(8,128)(2,1)S(1)} %get-tuple-element.72), channel_id=1, source_target_pairs={{0,2},{1,3},{2,0},{3,1},{4,6},{5,7},{6,4},{7,5},{8,10},{9,11},{10,... | collective-permute-start | bytes 393224 | tf_op jit(solution)/shard_map/ppermute | solution.py:220
  104.5 6.1 %collective-permute-start.11 = (bf16[64,512]{1,0:T(8,128)(2,1)S(1)}, bf16[64,512]{1,0:T(8,128)(2,1)S(1)}, u32[]{:S(2)}, u32[]{:S(2)}) collective-permute-start(bf16[64,512]{1,0:T(8,128)(2,1)S(1)} %get-tuple-element.48), channel_id=1, source_target_pairs={{0,2},{1,3},{2,0},{3,1},{4,6},{5,7},{6,4},{7,5},{8,10},{9,11},{10,... | collective-permute-start | bytes 196616 | tf_op jit(solution)/shard_map/ppermute | solution.py:220
  105.3 6.8 %collective-permute-start.16 = (bf16[64,512]{1,0:T(8,128)(2,1)S(1)}, bf16[64,512]{1,0:T(8,128)(2,1)S(1)}, u32[]{:S(2)}, u32[]{:S(2)}) collective-permute-start(bf16[64,512]{1,0:T(8,128)(2,1)S(1)} %get-tuple-element.56), channel_id=1, source_target_pairs={{0,2},{1,3},{2,0},{3,1},{4,6},{5,7},{6,4},{7,5},{8,10},{9,11},{10,... | collective-permute-start | bytes 196616 | tf_op jit(solution)/shard_map/ppermute | solution.py:220
  106.8 5.3 %collective-permute-start.24 = (bf16[64,512]{1,0:T(8,128)(2,1)S(1)}, bf16[64,512]{1,0:T(8,128)(2,1)S(1)}, u32[]{:S(2)}, u32[]{:S(2)}) collective-permute-start(bf16[64,512]{1,0:T(8,128)(2,1)S(1)} %get-tuple-element.64), channel_id=1, source_target_pairs={{0,2},{1,3},{2,0},{3,1},{4,6},{5,7},{6,4},{7,5},{8,10},{9,11},{10,... | collective-permute-start | bytes 196616 | tf_op jit(solution)/shard_map/ppermute | solution.py:220
  107.5 4.6 %collective-permute-start.27 = (bf16[64,512]{1,0:T(8,128)(2,1)S(1)}, bf16[64,512]{1,0:T(8,128)(2,1)S(1)}, u32[]{:S(2)}, u32[]{:S(2)}) collective-permute-start(bf16[64,512]{1,0:T(8,128)(2,1)S(1)} %get-tuple-element.71), channel_id=1, source_target_pairs={{0,4},{1,5},{2,6},{3,7},{4,0},{5,1},{6,2},{7,3},{8,12},{9,13},{10,... | collective-permute-start | bytes 196616 | tf_op jit(solution)/shard_map/ppermute | solution.py:220
  108.9 5.9 %collective-permute-start.29 = (bf16[64,512]{1,0:T(8,128)(2,1)S(1)}, bf16[64,512]{1,0:T(8,128)(2,1)S(1)}, u32[]{:S(2)}, u32[]{:S(2)}) collective-permute-start(bf16[64,512]{1,0:T(8,128)(2,1)S(1)} %get-tuple-element.75), channel_id=1, source_target_pairs={{0,8},{1,9},{2,10},{3,11},{4,12},{5,13},{6,14},{7,15},{8,0},{9,1},... | collective-permute-start | bytes 196616 | tf_op jit(solution)/shard_map/ppermute | solution.py:220
  110.6 6.1 %collective-permute-start.30 = (bf16[64,512]{1,0:T(8,128)(2,1)S(1)}, bf16[64,512]{1,0:T(8,128)(2,1)S(1)}, u32[]{:S(2)}, u32[]{:S(2)}) collective-permute-start(bf16[64,512]{1,0:T(8,128)(2,1)S(1)} %get-tuple-element.76), channel_id=1, source_target_pairs={{0,12},{1,13},{2,14},{3,15},{4,8},{5,9},{6,10},{7,11},{8,4},{9,5},... | collective-permute-start | bytes 196616 | tf_op jit(solution)/shard_map/ppermute | solution.py:220
  (8 other events, 16.8 us)

commit v2 on v1

--- a/solution.py
+++ b/solution.py
@@ -11,6 +11,7 @@
 AXES = ("grp", "vec", "occ", "wlk")
 HALVES = 2
 LOADS = 4
+LARGE = pltpu.CompilerParams(vmem_limit_bytes=44 * 2**20)
 SMALL = pltpu.CompilerParams(vmem_limit_bytes=24 * 2**20)
 
 
@@ -41,7 +42,8 @@
 def peer(position, hop, shards, back=False):
     if shards & (shards - 1) == 0:
         return position ^ hop
-    return (position + (shards - hop if back else hop)) % shards
+    moved = position + (shards - hop if back else hop)
+    return moved % shards if isinstance(moved, int) else lax.rem(moved, shards)
 
 
 def load_body(first, source, out, arrived):
@@ -53,11 +55,11 @@
 def loaded(factors, first, count):
     return pl.pallas_call(
         functools.partial(load_body, first),
-        in_specs=[pl.BlockSpec(memory_space=pl.ANY)],
+        in_specs=[pl.BlockSpec(memory_space=pltpu.HBM)],
         out_specs=VMEM,
         out_shape=pltpu.VMEM((count, factors.shape[1]), factors.dtype),
         scratch_shapes=[pltpu.SemaphoreType.DMA],
-        compiler_params=SMALL,
+        compiler_params=LARGE,
     )(factors)
 
 
@@ -65,7 +67,7 @@
     factors, pieces, own, far, rows = refs[:loads], refs[loads:-3], refs[-3], refs[-2], refs[-1]
     owned, width = pieces[0].shape[0], own.shape[1]
     for step in range(shards):
-        at = pl.multiple_of(place[step] * owned, owned)
+        at = pl.multiple_of(peer(place[0], step, shards, True) * owned, owned)
         if len(pieces) == shards:
             rows[pl.ds(at, owned), :] = pieces[step][...]
         else:
@@ -110,7 +112,7 @@
         at += len(vectors)
     owned = sums.shape[1] // shards
     for hop in range(shards):
-        low = pl.multiple_of(place[shards + hop] * owned, owned)
+        low = pl.multiple_of(peer(place[0], hop, shards) * owned, owned)
         if groups is None:
             outs[hop][...] = sums[:, pl.ds(low, owned)].astype(outs[hop].dtype)
             continue
@@ -200,7 +202,7 @@
     vectors, width, orbitals = chol_half.shape
     walkers = theta.shape[0]
     position = lax.axis_index("vec")
-    place = jnp.stack([peer(position, hop, shards, True) for hop in range(shards)] + [peer(position, hop, shards) for hop in range(shards)])
+    place = position.reshape(1)
     whole = chol_half.reshape(vectors * width, orbitals)
     factors = []
     for load in range(LOADS):

time: 118 us -> 119 us (level)
  local copies, waits for them, and re-layouts: 23.6 us -> 17.7 us
  Pallas kernels: 26.6 us -> 29.9 us
  waiting for transfers between devices: 22.3 us -> 25.5 us
    pallas_call x4, Pallas kernels: 1.16 us -> 8.78 us  [loaded(): pl.pallas_call(functools.partial(load_body, first), in_specs=[pl.BlockSpe...]
    unnamed x18 -> x16, local copies, waits for them, and re-layouts: 22.5 us -> 16.7 us
    ppermute x31, waiting for transfers between devices: 22.3 us -> 25.5 us  [moved(): return lax.ppermute(value, AXES, pairs)]
    pallas_call x4, Pallas kernels: 12 us -> 9.83 us  [amplitudes_of(): pl.pallas_call(functools.partial(amplitude_body, shards, len(factors), ha...]
    pallas_call x4, Pallas kernels: 12.3 us -> 10.1 us  [gradients_of(): pl.pallas_call(functools.partial(gradient_body, shards, len(factors), gro...]
  transfers between devices with their start and end apart: 31 -> 31, of which waited for: 8 -> 8; matrix products, arithmetic and copies ran while one was open for 1% -> 1% of each run, Pallas kernels for 22% -> 24%
where the time goes in v2:
time: 119 us; the launch traced here: 118 us
  starting transfers between devices  44.9 us (38%)
  Pallas kernels  29.9 us (25%)
  waiting for transfers between devices  25.5 us (21%)
  local copies, waits for them, and re-layouts  17.7 us (15%)
    ppermute x31, starting transfers between devices, moved(): return lax.ppermute(value, AXES, pairs)  44.9 us
    ppermute x31, waiting for transfers between devices, moved(): return lax.ppermute(value, AXES, pairs)  25.5 us
    unnamed x16, local copies, waits for them, and re-layouts  16.7 us
    pallas_call x4, Pallas kernels, gradients_of(): pl.pallas_call(functools.partial(gradient_body, shards, len(factors), gro...  10.1 us
    pallas_call x4, Pallas kernels, amplitudes_of(): pl.pallas_call(functools.partial(amplitude_body, shards, len(factors), ha...  9.83 us
    pallas_call x4, Pallas kernels, loaded(): pl.pallas_call(functools.partial(load_body, first), in_specs=[pl.BlockSpe...  8.78 us
  transfers between devices with their start and end apart: 31, of which 8 were waited for; matrix products, arithmetic and copies ran while one was open for 1% of the time, Pallas kernels for 24%

profile of v2, /device:TPU:0, one launch (start us, length us, event | category | flops | bytes accessed | tf_op | source)
XLA Modules:
  0.0 118.3 jit_solution(15599449486331475049)
XLA Ops:
  0.0 3.0 %collective-permute-start.3 = (bf16[2,512,128]{2,1,0:T(8,128)(2,1)}, bf16[2,512,128]{2,1,0:T(8,128)(2,1)S(1)}, u32[]{:S(2)}, u32[]{:S(2)}) collective-permute-start(bf16[2,512,128]{2,1,0:T(8,128)(2,1)} %param.3), channel_id=1, source_target_pairs={{0,2},{1,3},{2,0},{3,1},{4,6},{5,7},{6,4},{7,5},{8,10},{9,11},{10,... | collective-permute-start | bytes 786440 | tf_op jit(solution)/shard_map/ppermute | solution.py:222
  5.6 2.6 %collective-permute-start.1 = (bf16[512,128]{1,0:T(8,128)(2,1)S(1)}, bf16[512,128]{1,0:T(8,128)(2,1)S(1)}, u32[]{:S(2)}, u32[]{:S(2)}) collective-permute-start(bf16[512,128]{1,0:T(8,128)(2,1)S(1)} %get-tuple-element.78.refs_4_), channel_id=1, source_target_pairs={{0,8},{1,9},{2,10},{3,11},{4,12},{5,13},{6,14},{7,15},{8,0},{9,1},... | collective-permute-start | bytes 393224 | tf_op jit(solution)/shard_map/ppermute | solution.py:222
  8.4 2.2 %shard_map.28.refs_0_ = bf16[1024,2048]{1,0:T(8,128)(2,1)S(1)} custom-call(bf16[4096,2048]{1,0:T(8,128)(2,1)} %bitcast.10), custom_call_target="tpu_custom_call" | custom-call | tf_op jit(solution)/shard_map/pallas_call | solution.py:56
  10.6 2.0 %copy-done = bf16[1024,2048]{1,0:T(8,128)(2,1)} copy-done((bf16[1024,2048]{1,0:T(8,128)(2,1)}, bf16[1024,2048]{1,0:T(8,128)(2,1)S(1)}, u32[]{:S(2)}) %copy-start) | copy-done | bytes 4194328
  12.6 2.2 %shard_map.29.refs_1_ = bf16[1024,2048]{1,0:T(8,128)(2,1)S(1)} custom-call(bf16[4096,2048]{1,0:T(8,128)(2,1)} %bitcast.11), custom_call_target="tpu_custom_call" | custom-call | tf_op jit(solution)/shard_map/pallas_call | solution.py:56
  14.8 2.0 %copy-done.2 = bf16[1024,2048]{1,0:T(8,128)(2,1)} copy-done((bf16[1024,2048]{1,0:T(8,128)(2,1)}, bf16[1024,2048]{1,0:T(8,128)(2,1)S(1)}, u32[]{:S(2)}) %copy-start.2) | copy-done | bytes 4194328
  16.8 2.2 %shard_map.30.refs_2_ = bf16[1024,2048]{1,0:T(8,128)(2,1)S(1)} custom-call(bf16[4096,2048]{1,0:T(8,128)(2,1)} %bitcast.12), custom_call_target="tpu_custom_call" | custom-call | tf_op jit(solution)/shard_map/pallas_call | solution.py:56
  19.0 2.1 %copy-done.4 = bf16[1024,2048]{1,0:T(8,128)(2,1)} copy-done((bf16[1024,2048]{1,0:T(8,128)(2,1)}, bf16[1024,2048]{1,0:T(8,128)(2,1)S(1)}, u32[]{:S(2)}) %copy-start.4) | copy-done | bytes 4194328
  21.1 2.2 %shard_map.31.refs_3_ = bf16[1024,2048]{1,0:T(8,128)(2,1)S(1)} custom-call(bf16[4096,2048]{1,0:T(8,128)(2,1)} %bitcast.13), custom_call_target="tpu_custom_call" | custom-call | tf_op jit(solution)/shard_map/pallas_call | solution.py:56
  28.6 3.5 %collective-permute-start.18 = (bf16[512,256]{1,0:T(8,128)(2,1)S(1)}, bf16[512,256]{1,0:T(8,128)(2,1)S(1)}, u32[]{:S(2)}, u32[]{:S(2)}) collective-permute-start(bf16[512,256]{1,0:T(8,128)(2,1)S(1)} %pad_maximum_fusion.refs_4_), channel_id=1, source_target_pairs={{0,8},{1,9},{2,10},{3,11},{4,12},{5,13},{6,14},{7,15},{8,0},{9,1},... | collective-permute-start | bytes 786440 | tf_op jit(solution)/shard_map/ppermute | solution.py:222
  32.1 3.1 %collective-permute-start.19 = (bf16[512,256]{1,0:T(8,128)(2,1)S(1)}, bf16[512,256]{1,0:T(8,128)(2,1)S(1)}, u32[]{:S(2)}, u32[]{:S(2)}) collective-permute-start(bf16[512,256]{1,0:T(8,128)(2,1)S(1)} %pad_maximum_fusion.refs_4_), channel_id=1, source_target_pairs={{0,12},{1,13},{2,14},{3,15},{4,8},{5,9},{6,10},{7,11},{8,4},{9,5},... | collective-permute-start | bytes 786440 | tf_op jit(solution)/shard_map/ppermute | solution.py:222
  35.2 2.2 %copy-done.1 = bf16[1024,2048]{1,0:T(8,128)(2,1)S(1)} copy-done((bf16[1024,2048]{1,0:T(8,128)(2,1)S(1)}, bf16[1024,2048]{1,0:T(8,128)(2,1)}, u32[]{:S(2)}) %copy-start.1) | copy-done | bytes 4194328
  37.4 2.2 %copy-done.3 = bf16[1024,2048]{1,0:T(8,128)(2,1)S(1)} copy-done((bf16[1024,2048]{1,0:T(8,128)(2,1)S(1)}, bf16[1024,2048]{1,0:T(8,128)(2,1)}, u32[]{:S(2)}) %copy-start.3) | copy-done | bytes 4194328
  39.6 2.2 %copy-done.5 = bf16[1024,2048]{1,0:T(8,128)(2,1)S(1)} copy-done((bf16[1024,2048]{1,0:T(8,128)(2,1)S(1)}, bf16[1024,2048]{1,0:T(8,128)(2,1)}, u32[]{:S(2)}) %copy-start.5) | copy-done | bytes 4194328
  41.8 2.2 %copy-done.7 = bf16[1024,2048]{1,0:T(8,128)(2,1)S(1)} copy-done((bf16[1024,2048]{1,0:T(8,128)(2,1)S(1)}, bf16[1024,2048]{1,0:T(8,128)(2,1)}, u32[]{:S(2)}) %copy-start.7) | copy-done | bytes 4194328
  44.0 2.5 %shard_map.32 = (bf16[2048,128]{1,0:T(8,128)(2,1)S(1)}, bf16[2048,128]{1,0:T(8,128)(2,1)S(1)}) custom-call(s32[1]{0:T(128)} %bitcast.place, bf16[1024,2048]{1,0:T(8,128)(2,1)S(1)} %copy-done.1, bf16[1024,2048]{1,0:T(8,128)(2,1)S(1)} %copy-done.3, bf16[1024,2048]{1,0:T(8,128)(2,1)S(1)} %copy-done.5, bf16[1024,2048]{1,0:T(8,128)(2,1)S(1)} %copy-done.7, ...), custom_call_target="tpu_custom_call" | custom-call | flops 2147483648 | bytes 8388608 | tf_op jit(solution)/shard_map/pallas_call | solution.py:89
  47.1 2.5 %shard_map.35 = (bf16[2048,128]{1,0:T(8,128)(2,1)S(1)}, bf16[2048,128]{1,0:T(8,128)(2,1)S(1)}) custom-call(s32[1]{0:T(128)} %bitcast.place, bf16[1024,2048]{1,0:T(8,128)(2,1)S(1)} %copy-done.1, bf16[1024,2048]{1,0:T(8,128)(2,1)S(1)} %copy-done.3, bf16[1024,2048]{1,0:T(8,128)(2,1)S(1)} %copy-done.5, bf16[1024,2048]{1,0:T(8,128)(2,1)S(1)} %copy-done.7, ...), custom_call_target="tpu_custom_call" | custom-call | flops 2147483648 | bytes 8388608 | tf_op jit(solution)/shard_map/pallas_call | solution.py:89
  51.2 2.4 %shard_map.38 = (bf16[2048,128]{1,0:T(8,128)(2,1)S(1)}, bf16[2048,128]{1,0:T(8,128)(2,1)S(1)}) custom-call(s32[1]{0:T(128)} %bitcast.place, bf16[1024,2048]{1,0:T(8,128)(2,1)S(1)} %copy-done.1, bf16[1024,2048]{1,0:T(8,128)(2,1)S(1)} %copy-done.3, bf16[1024,2048]{1,0:T(8,128)(2,1)S(1)} %copy-done.5, bf16[1024,2048]{1,0:T(8,128)(2,1)S(1)} %copy-done.7, ...), custom_call_target="tpu_custom_call" | custom-call | flops 2147483648 | bytes 8388608 | tf_op jit(solution)/shard_map/pallas_call | solution.py:89
  54.2 2.4 %shard_map.41 = (bf16[2048,128]{1,0:T(8,128)(2,1)S(1)}, bf16[2048,128]{1,0:T(8,128)(2,1)S(1)}) custom-call(s32[1]{0:T(128)} %bitcast.place, bf16[1024,2048]{1,0:T(8,128)(2,1)S(1)} %copy-done.1, bf16[1024,2048]{1,0:T(8,128)(2,1)S(1)} %copy-done.3, bf16[1024,2048]{1,0:T(8,128)(2,1)S(1)} %copy-done.5, bf16[1024,2048]{1,0:T(8,128)(2,1)S(1)} %copy-done.7, ...), custom_call_target="tpu_custom_call" | custom-call | flops 2147483648 | bytes 8388608 | tf_op jit(solution)/shard_map/pallas_call | solution.py:89
  58.1 3.2 %collective-permute-done.7.far = bf16[2048,128]{1,0:T(8,128)(2,1)S(1)} collective-permute-done((bf16[2048,128]{1,0:T(8,128)(2,1)S(1)}, bf16[2048,128]{1,0:T(8,128)(2,1)S(1)}, u32[]{:S(2)}, u32[]{:S(2)}) %collective-permute-start.7) | collective-permute-done | bytes 524320 | tf_op jit(solution)/shard_map/ppermute | solution.py:222
  61.3 2.5 %shard_map.33 = (f32[128,512]{1,0:T(8,128)S(1)}, bf16[128,512]{1,0:T(8,128)(2,1)S(1)}, bf16[128,512]{1,0:T(8,128)(2,1)S(1)}, bf16[128,512]{1,0:T(8,128)(2,1)S(1)}) custom-call(s32[1]{0:T(128)} %bitcast.place, bf16[2048,128]{1,0:T(8,128)(2,1)S(1)} %get-tuple-element.41.own, bf16[2048,128]{1,0:T(8,128)(2,1)S(1)} %collective-permute-done.7.far, ...), custom_call_target="tpu_custom_call" | custom-call | flops 2147483648 | bytes 16777216 | tf_op jit(solution)/shard_map/pallas_call | solution.py:135
  64.3 3.5 %collective-permute-start.9 = (bf16[128,512]{1,0:T(8,128)(2,1)S(1)}, bf16[128,512]{1,0:T(8,128)(2,1)S(1)}, u32[]{:S(2)}, u32[]{:S(2)}) collective-permute-start(bf16[128,512]{1,0:T(8,128)(2,1)S(1)} %get-tuple-element.45), channel_id=1, source_target_pairs={{0,8},{1,9},{2,10},{3,11},{4,12},{5,13},{6,14},{7,15},{8,0},{9,1},... | collective-permute-start | bytes 393224 | tf_op jit(solution)/shard_map/ppermute | solution.py:222
  67.8 4.8 %collective-permute-done.12.far = bf16[2048,128]{1,0:T(8,128)(2,1)S(1)} collective-permute-done((bf16[2048,128]{1,0:T(8,128)(2,1)S(1)}, bf16[2048,128]{1,0:T(8,128)(2,1)S(1)}, u32[]{:S(2)}, u32[]{:S(2)}) %collective-permute-start.12) | collective-permute-done | bytes 524320 | tf_op jit(solution)/shard_map/ppermute | solution.py:222
  72.6 3.4 %collective-permute-start.10 = (bf16[128,512]{1,0:T(8,128)(2,1)S(1)}, bf16[128,512]{1,0:T(8,128)(2,1)S(1)}, u32[]{:S(2)}, u32[]{:S(2)}) collective-permute-start(bf16[128,512]{1,0:T(8,128)(2,1)S(1)} %get-tuple-element.46), channel_id=1, source_target_pairs={{0,12},{1,13},{2,14},{3,15},{4,8},{5,9},{6,10},{7,11},{8,4},{9,5},... | collective-permute-start | bytes 393224 | tf_op jit(solution)/shard_map/ppermute | solution.py:222
  75.9 2.7 %shard_map.36 = (f32[128,512]{1,0:T(8,128)S(1)}, bf16[128,512]{1,0:T(8,128)(2,1)S(1)}, bf16[128,512]{1,0:T(8,128)(2,1)S(1)}, bf16[128,512]{1,0:T(8,128)(2,1)S(1)}) custom-call(s32[1]{0:T(128)} %bitcast.place, bf16[2048,128]{1,0:T(8,128)(2,1)S(1)} %get-tuple-element.49.own, bf16[2048,128]{1,0:T(8,128)(2,1)S(1)} %collective-permute-done.12.far, ...), custom_call_target="tpu_custom_call" | custom-call | flops 2147483648 | bytes 16777216 | tf_op jit(solution)/shard_map/pallas_call | solution.py:135
  78.6 5.2 %collective-permute-done.20.far = bf16[2048,128]{1,0:T(8,128)(2,1)S(1)} collective-permute-done((bf16[2048,128]{1,0:T(8,128)(2,1)S(1)}, bf16[2048,128]{1,0:T(8,128)(2,1)S(1)}, u32[]{:S(2)}, u32[]{:S(2)}) %collective-permute-start.20) | collective-permute-done | bytes 524320 | tf_op jit(solution)/shard_map/ppermute | solution.py:222
  84.2 2.5 %shard_map.39 = (f32[128,512]{1,0:T(8,128)S(1)}, bf16[128,512]{1,0:T(8,128)(2,1)S(1)}, bf16[128,512]{1,0:T(8,128)(2,1)S(1)}, bf16[128,512]{1,0:T(8,128)(2,1)S(1)}) custom-call(s32[1]{0:T(128)} %bitcast.place, bf16[2048,128]{1,0:T(8,128)(2,1)S(1)} %get-tuple-element.57.own, bf16[2048,128]{1,0:T(8,128)(2,1)S(1)} %collective-permute-done.20.far, ...), custom_call_target="tpu_custom_call" | custom-call | flops 2147483648 | bytes 16777216 | tf_op jit(solution)/shard_map/pallas_call | solution.py:135
  86.7 3.6 %collective-permute-start.14 = (bf16[128,512]{1,0:T(8,128)(2,1)S(1)}, bf16[128,512]{1,0:T(8,128)(2,1)S(1)}, u32[]{:S(2)}, u32[]{:S(2)}) collective-permute-start(bf16[128,512]{1,0:T(8,128)(2,1)S(1)} %get-tuple-element.53), channel_id=1, source_target_pairs={{0,8},{1,9},{2,10},{3,11},{4,12},{5,13},{6,14},{7,15},{8,0},{9,1},... | collective-permute-start | bytes 393224 | tf_op jit(solution)/shard_map/ppermute | solution.py:222
  90.9 2.4 %collective-permute-done.13.refs_1_ = bf16[128,512]{1,0:T(8,128)(2,1)S(1)} collective-permute-done((bf16[128,512]{1,0:T(8,128)(2,1)S(1)}, bf16[128,512]{1,0:T(8,128)(2,1)S(1)}, u32[]{:S(2)}, u32[]{:S(2)}) %collective-permute-start.13) | collective-permute-done | bytes 131104 | tf_op jit(solution)/shard_map/ppermute | solution.py:222
  95.4 2.5 %shard_map.42 = (f32[64,512]{1,0:T(8,128)S(1)}, f32[64,512]{1,0:T(8,128)S(1)}, f32[64,512]{1,0:T(8,128)S(1)}, f32[64,512]{1,0:T(8,128)S(1)}, bf16[64,1024]{1,0:T(8,128)(2,1)S(1)}, /*index=5*/bf16[64,1024]{1,0:T(8,128)(2,1)S(1)}) custom-call(s32[1]{0:T(128)} %bitcast.place, bf16[2048,128]{1,0:T(8,128)(2,1)S(1)} %get-tuple-element.65.own, ...), custom_call_target="tpu_custom_call" | custom-call | flops 2147483648 | bytes 16777216 | tf_op jit(solution)/shard_map/pallas_call | solution.py:135
  97.9 5.1 %collective-permute-done.14.refs_2_ = bf16[128,512]{1,0:T(8,128)(2,1)S(1)} collective-permute-done((bf16[128,512]{1,0:T(8,128)(2,1)S(1)}, bf16[128,512]{1,0:T(8,128)(2,1)S(1)}, u32[]{:S(2)}, u32[]{:S(2)}) %collective-permute-start.14) | collective-permute-done | bytes 131104 | tf_op jit(solution)/shard_map/ppermute | solution.py:222
  112.7 2.8 %collective-permute-done.29.refs_8_ = bf16[64,512]{1,0:T(8,128)(2,1)S(1)} collective-permute-done((bf16[64,512]{1,0:T(8,128)(2,1)S(1)}, bf16[64,512]{1,0:T(8,128)(2,1)S(1)}, u32[]{:S(2)}, u32[]{:S(2)}) %collective-permute-start.29) | collective-permute-done | bytes 65568 | tf_op jit(solution)/shard_map/ppermute | solution.py:222
  (67 shorter events, 28.5 us)
Async XLA Ops:
  0.0 27.6 %collective-permute-start.3 = (bf16[2,512,128]{2,1,0:T(8,128)(2,1)}, bf16[2,512,128]{2,1,0:T(8,128)(2,1)S(1)}, u32[]{:S(2)}, u32[]{:S(2)}) collective-permute-start(bf16[2,512,128]{2,1,0:T(8,128)(2,1)} %param.3), channel_id=1, source_target_pairs={{0,2},{1,3},{2,0},{3,1},{4,6},{5,7},{6,4},{7,5},{8,10},{9,11},{10,... | collective-permute-start | bytes 786440 | tf_op jit(solution)/shard_map/ppermute | solution.py:222
  4.0 21.3 %collective-permute-start = (bf16[512,128]{1,0:T(8,128)(2,1)S(1)}, bf16[512,128]{1,0:T(8,128)(2,1)S(1)}, u32[]{:S(2)}, u32[]{:S(2)}) collective-permute-start(bf16[512,128]{1,0:T(8,128)(2,1)S(1)} %get-tuple-element.78.refs_4_), channel_id=1, source_target_pairs={{0,4},{1,5},{2,6},{3,7},{4,0},{5,1},{6,2},{7,3},{8,12},{9,13},{10,... | collective-permute-start | bytes 393224 | tf_op jit(solution)/shard_map/ppermute | solution.py:222
  5.6 19.9 %collective-permute-start.1 = (bf16[512,128]{1,0:T(8,128)(2,1)S(1)}, bf16[512,128]{1,0:T(8,128)(2,1)S(1)}, u32[]{:S(2)}, u32[]{:S(2)}) collective-permute-start(bf16[512,128]{1,0:T(8,128)(2,1)S(1)} %get-tuple-element.78.refs_4_), channel_id=1, source_target_pairs={{0,8},{1,9},{2,10},{3,11},{4,12},{5,13},{6,14},{7,15},{8,0},{9,1},... | collective-permute-start | bytes 393224 | tf_op jit(solution)/shard_map/ppermute | solution.py:222
  8.2 19.1 %collective-permute-start.2 = (bf16[512,128]{1,0:T(8,128)(2,1)S(1)}, bf16[512,128]{1,0:T(8,128)(2,1)S(1)}, u32[]{:S(2)}, u32[]{:S(2)}) collective-permute-start(bf16[512,128]{1,0:T(8,128)(2,1)S(1)} %get-tuple-element.78.refs_4_), channel_id=1, source_target_pairs={{0,12},{1,13},{2,14},{3,15},{4,8},{5,9},{6,10},{7,11},{8,4},{9,5},... | collective-permute-start | bytes 393224 | tf_op jit(solution)/shard_map/ppermute | solution.py:222
  25.2 6.9 %collective-permute-start.4 = (bf16[512,128]{1,0:T(8,128)(2,1)S(1)}, bf16[512,128]{1,0:T(8,128)(2,1)S(1)}, u32[]{:S(2)}, u32[]{:S(2)}) collective-permute-start(bf16[512,128]{1,0:T(8,128)(2,1)S(1)} %collective-permute-done.refs_5_), channel_id=1, source_target_pairs={{0,2},{1,3},{2,0},{3,1},{4,6},{5,7},{6,4},{7,5},{8,10},{9,11},{10,... | collective-permute-start | bytes 393224 | tf_op jit(solution)/shard_map/ppermute | solution.py:222
  25.5 9.7 %collective-permute-start.5 = (bf16[512,128]{1,0:T(8,128)(2,1)S(1)}, bf16[512,128]{1,0:T(8,128)(2,1)S(1)}, u32[]{:S(2)}, u32[]{:S(2)}) collective-permute-start(bf16[512,128]{1,0:T(8,128)(2,1)S(1)} %collective-permute-done.1.refs_6_), channel_id=1, source_target_pairs={{0,2},{1,3},{2,0},{3,1},{4,6},{5,7},{6,4},{7,5},{8,10},{9,11},{10,... | collective-permute-start | bytes 393224 | tf_op jit(solution)/shard_map/ppermute | solution.py:222
  27.3 7.9 %collective-permute-start.6 = (bf16[512,128]{1,0:T(8,128)(2,1)S(1)}, bf16[512,128]{1,0:T(8,128)(2,1)S(1)}, u32[]{:S(2)}, u32[]{:S(2)}) collective-permute-start(bf16[512,128]{1,0:T(8,128)(2,1)S(1)} %collective-permute-done.2.refs_7_), channel_id=1, source_target_pairs={{0,2},{1,3},{2,0},{3,1},{4,6},{5,7},{6,4},{7,5},{8,10},{9,11},{10,... | collective-permute-start | bytes 393224 | tf_op jit(solution)/shard_map/ppermute | solution.py:222
  27.6 23.5 %collective-permute-start.17 = (bf16[512,256]{1,0:T(8,128)(2,1)S(1)}, bf16[512,256]{1,0:T(8,128)(2,1)S(1)}, u32[]{:S(2)}, u32[]{:S(2)}) collective-permute-start(bf16[512,256]{1,0:T(8,128)(2,1)S(1)} %pad_maximum_fusion.refs_4_), channel_id=1, source_target_pairs={{0,4},{1,5},{2,6},{3,7},{4,0},{5,1},{6,2},{7,3},{8,12},{9,13},{10,... | collective-permute-start | bytes 786440 | tf_op jit(solution)/shard_map/ppermute | solution.py:222
  28.6 22.6 %collective-permute-start.18 = (bf16[512,256]{1,0:T(8,128)(2,1)S(1)}, bf16[512,256]{1,0:T(8,128)(2,1)S(1)}, u32[]{:S(2)}, u32[]{:S(2)}) collective-permute-start(bf16[512,256]{1,0:T(8,128)(2,1)S(1)} %pad_maximum_fusion.refs_4_), channel_id=1, source_target_pairs={{0,8},{1,9},{2,10},{3,11},{4,12},{5,13},{6,14},{7,15},{8,0},{9,1},... | collective-permute-start | bytes 786440 | tf_op jit(solution)/shard_map/ppermute | solution.py:222
  32.1 19.1 %collective-permute-start.19 = (bf16[512,256]{1,0:T(8,128)(2,1)S(1)}, bf16[512,256]{1,0:T(8,128)(2,1)S(1)}, u32[]{:S(2)}, u32[]{:S(2)}) collective-permute-start(bf16[512,256]{1,0:T(8,128)(2,1)S(1)} %pad_maximum_fusion.refs_4_), channel_id=1, source_target_pairs={{0,12},{1,13},{2,14},{3,15},{4,8},{5,9},{6,10},{7,11},{8,4},{9,5},... | collective-permute-start | bytes 786440 | tf_op jit(solution)/shard_map/ppermute | solution.py:222
  35.2 2.2 %copy-start.1 = (bf16[1024,2048]{1,0:T(8,128)(2,1)S(1)}, bf16[1024,2048]{1,0:T(8,128)(2,1)}, u32[]{:S(2)}) copy-start(bf16[1024,2048]{1,0:T(8,128)(2,1)} %copy-done) | copy-start | bytes 12582916
  46.5 14.9 %collective-permute-start.7 = (bf16[2048,128]{1,0:T(8,128)(2,1)S(1)}, bf16[2048,128]{1,0:T(8,128)(2,1)S(1)}, u32[]{:S(2)}, u32[]{:S(2)}) collective-permute-start(bf16[2048,128]{1,0:T(8,128)(2,1)S(1)} %get-tuple-element.42), channel_id=1, source_target_pairs={{0,2},{1,3},{2,0},{3,1},{4,6},{5,7},{6,4},{7,5},{8,10},{9,11},{10,... | collective-permute-start | bytes 1572872 | tf_op jit(solution)/shard_map/ppermute | solution.py:222
  49.6 23.0 %collective-permute-start.12 = (bf16[2048,128]{1,0:T(8,128)(2,1)S(1)}, bf16[2048,128]{1,0:T(8,128)(2,1)S(1)}, u32[]{:S(2)}, u32[]{:S(2)}) collective-permute-start(bf16[2048,128]{1,0:T(8,128)(2,1)S(1)} %get-tuple-element.50), channel_id=1, source_target_pairs={{0,2},{1,3},{2,0},{3,1},{4,6},{5,7},{6,4},{7,5},{8,10},{9,11},{10,... | collective-permute-start | bytes 1572872 | tf_op jit(solution)/shard_map/ppermute | solution.py:222
  53.6 30.2 %collective-permute-start.20 = (bf16[2048,128]{1,0:T(8,128)(2,1)S(1)}, bf16[2048,128]{1,0:T(8,128)(2,1)S(1)}, u32[]{:S(2)}, u32[]{:S(2)}) collective-permute-start(bf16[2048,128]{1,0:T(8,128)(2,1)S(1)} %get-tuple-element.58), channel_id=1, source_target_pairs={{0,2},{1,3},{2,0},{3,1},{4,6},{5,7},{6,4},{7,5},{8,10},{9,11},{10,... | collective-permute-start | bytes 1572872 | tf_op jit(solution)/shard_map/ppermute | solution.py:222
  56.6 38.1 %collective-permute-start.25 = (bf16[2048,128]{1,0:T(8,128)(2,1)S(1)}, bf16[2048,128]{1,0:T(8,128)(2,1)S(1)}, u32[]{:S(2)}, u32[]{:S(2)}) collective-permute-start(bf16[2048,128]{1,0:T(8,128)(2,1)S(1)} %get-tuple-element.66), channel_id=1, source_target_pairs={{0,2},{1,3},{2,0},{3,1},{4,6},{5,7},{6,4},{7,5},{8,10},{9,11},{10,... | collective-permute-start | bytes 1572872 | tf_op jit(solution)/shard_map/ppermute | solution.py:222
  63.8 22.9 %collective-permute-start.8 = (bf16[128,512]{1,0:T(8,128)(2,1)S(1)}, bf16[128,512]{1,0:T(8,128)(2,1)S(1)}, u32[]{:S(2)}, u32[]{:S(2)}) collective-permute-start(bf16[128,512]{1,0:T(8,128)(2,1)S(1)} %get-tuple-element.44), channel_id=1, source_target_pairs={{0,4},{1,5},{2,6},{3,7},{4,0},{5,1},{6,2},{7,3},{8,12},{9,13},{10,... | collective-permute-start | bytes 393224 | tf_op jit(solution)/shard_map/ppermute | solution.py:222
  64.3 26.0 %collective-permute-start.9 = (bf16[128,512]{1,0:T(8,128)(2,1)S(1)}, bf16[128,512]{1,0:T(8,128)(2,1)S(1)}, u32[]{:S(2)}, u32[]{:S(2)}) collective-permute-start(bf16[128,512]{1,0:T(8,128)(2,1)S(1)} %get-tuple-element.45), channel_id=1, source_target_pairs={{0,8},{1,9},{2,10},{3,11},{4,12},{5,13},{6,14},{7,15},{8,0},{9,1},... | collective-permute-start | bytes 393224 | tf_op jit(solution)/shard_map/ppermute | solution.py:222
  72.6 18.2 %collective-permute-start.10 = (bf16[128,512]{1,0:T(8,128)(2,1)S(1)}, bf16[128,512]{1,0:T(8,128)(2,1)S(1)}, u32[]{:S(2)}, u32[]{:S(2)}) collective-permute-start(bf16[128,512]{1,0:T(8,128)(2,1)S(1)} %get-tuple-element.46), channel_id=1, source_target_pairs={{0,12},{1,13},{2,14},{3,15},{4,8},{5,9},{6,10},{7,11},{8,4},{9,5},... | collective-permute-start | bytes 393224 | tf_op jit(solution)/shard_map/ppermute | solution.py:222
  83.8 9.6 %collective-permute-start.13 = (bf16[128,512]{1,0:T(8,128)(2,1)S(1)}, bf16[128,512]{1,0:T(8,128)(2,1)S(1)}, u32[]{:S(2)}, u32[]{:S(2)}) collective-permute-start(bf16[128,512]{1,0:T(8,128)(2,1)S(1)} %get-tuple-element.52), channel_id=1, source_target_pairs={{0,4},{1,5},{2,6},{3,7},{4,0},{5,1},{6,2},{7,3},{8,12},{9,13},{10,... | collective-permute-start | bytes 393224 | tf_op jit(solution)/shard_map/ppermute | solution.py:222
  86.7 16.3 %collective-permute-start.14 = (bf16[128,512]{1,0:T(8,128)(2,1)S(1)}, bf16[128,512]{1,0:T(8,128)(2,1)S(1)}, u32[]{:S(2)}, u32[]{:S(2)}) collective-permute-start(bf16[128,512]{1,0:T(8,128)(2,1)S(1)} %get-tuple-element.53), channel_id=1, source_target_pairs={{0,8},{1,9},{2,10},{3,11},{4,12},{5,13},{6,14},{7,15},{8,0},{9,1},... | collective-permute-start | bytes 393224 | tf_op jit(solution)/shard_map/ppermute | solution.py:222
  90.3 13.3 %collective-permute-start.15 = (bf16[128,512]{1,0:T(8,128)(2,1)S(1)}, bf16[128,512]{1,0:T(8,128)(2,1)S(1)}, u32[]{:S(2)}, u32[]{:S(2)}) collective-permute-start(bf16[128,512]{1,0:T(8,128)(2,1)S(1)} %get-tuple-element.54), channel_id=1, source_target_pairs={{0,12},{1,13},{2,14},{3,15},{4,8},{5,9},{6,10},{7,11},{8,4},{9,5},... | collective-permute-start | bytes 393224 | tf_op jit(solution)/shard_map/ppermute | solution.py:222
  90.8 14.3 %collective-permute-start.21 = (bf16[128,512]{1,0:T(8,128)(2,1)S(1)}, bf16[128,512]{1,0:T(8,128)(2,1)S(1)}, u32[]{:S(2)}, u32[]{:S(2)}) collective-permute-start(bf16[128,512]{1,0:T(8,128)(2,1)S(1)} %get-tuple-element.60), channel_id=1, source_target_pairs={{0,4},{1,5},{2,6},{3,7},{4,0},{5,1},{6,2},{7,3},{8,12},{9,13},{10,... | collective-permute-start | bytes 393224 | tf_op jit(solution)/shard_map/ppermute | solution.py:222
  93.4 12.5 %collective-permute-start.22 = (bf16[128,512]{1,0:T(8,128)(2,1)S(1)}, bf16[128,512]{1,0:T(8,128)(2,1)S(1)}, u32[]{:S(2)}, u32[]{:S(2)}) collective-permute-start(bf16[128,512]{1,0:T(8,128)(2,1)S(1)} %get-tuple-element.61), channel_id=1, source_target_pairs={{0,8},{1,9},{2,10},{3,11},{4,12},{5,13},{6,14},{7,15},{8,0},{9,1},... | collective-permute-start | bytes 393224 | tf_op jit(solution)/shard_map/ppermute | solution.py:222
  94.7 12.6 %collective-permute-start.23 = (bf16[128,512]{1,0:T(8,128)(2,1)S(1)}, bf16[128,512]{1,0:T(8,128)(2,1)S(1)}, u32[]{:S(2)}, u32[]{:S(2)}) collective-permute-start(bf16[128,512]{1,0:T(8,128)(2,1)S(1)} %get-tuple-element.62), channel_id=1, source_target_pairs={{0,12},{1,13},{2,14},{3,15},{4,8},{5,9},{6,10},{7,11},{8,4},{9,5},... | collective-permute-start | bytes 393224 | tf_op jit(solution)/shard_map/ppermute | solution.py:222
  103.0 5.1 %collective-permute-start.26 = (bf16[64,1024]{1,0:T(8,128)(2,1)S(1)}, bf16[64,1024]{1,0:T(8,128)(2,1)S(1)}, u32[]{:S(2)}, u32[]{:S(2)}) collective-permute-start(bf16[64,1024]{1,0:T(8,128)(2,1)S(1)} %get-tuple-element.67), channel_id=1, source_target_pairs={{0,2},{1,3},{2,0},{3,1},{4,6},{5,7},{6,4},{7,5},{8,10},{9,11},{10,... | collective-permute-start | bytes 393224 | tf_op jit(solution)/shard_map/ppermute | solution.py:222
  103.6 5.9 %collective-permute-start.28 = (bf16[64,1024]{1,0:T(8,128)(2,1)S(1)}, bf16[64,1024]{1,0:T(8,128)(2,1)S(1)}, u32[]{:S(2)}, u32[]{:S(2)}) collective-permute-start(bf16[64,1024]{1,0:T(8,128)(2,1)S(1)} %get-tuple-element.72), channel_id=1, source_target_pairs={{0,2},{1,3},{2,0},{3,1},{4,6},{5,7},{6,4},{7,5},{8,10},{9,11},{10,... | collective-permute-start | bytes 393224 | tf_op jit(solution)/shard_map/ppermute | solution.py:222
  105.1 6.1 %collective-permute-start.11 = (bf16[64,512]{1,0:T(8,128)(2,1)S(1)}, bf16[64,512]{1,0:T(8,128)(2,1)S(1)}, u32[]{:S(2)}, u32[]{:S(2)}) collective-permute-start(bf16[64,512]{1,0:T(8,128)(2,1)S(1)} %get-tuple-element.48), channel_id=1, source_target_pairs={{0,2},{1,3},{2,0},{3,1},{4,6},{5,7},{6,4},{7,5},{8,10},{9,11},{10,... | collective-permute-start | bytes 196616 | tf_op jit(solution)/shard_map/ppermute | solution.py:222
  105.9 6.8 %collective-permute-start.16 = (bf16[64,512]{1,0:T(8,128)(2,1)S(1)}, bf16[64,512]{1,0:T(8,128)(2,1)S(1)}, u32[]{:S(2)}, u32[]{:S(2)}) collective-permute-start(bf16[64,512]{1,0:T(8,128)(2,1)S(1)} %get-tuple-element.56), channel_id=1, source_target_pairs={{0,2},{1,3},{2,0},{3,1},{4,6},{5,7},{6,4},{7,5},{8,10},{9,11},{10,... | collective-permute-start | bytes 196616 | tf_op jit(solution)/shard_map/ppermute | solution.py:222
  107.4 5.3 %collective-permute-start.24 = (bf16[64,512]{1,0:T(8,128)(2,1)S(1)}, bf16[64,512]{1,0:T(8,128)(2,1)S(1)}, u32[]{:S(2)}, u32[]{:S(2)}) collective-permute-start(bf16[64,512]{1,0:T(8,128)(2,1)S(1)} %get-tuple-element.64), channel_id=1, source_target_pairs={{0,2},{1,3},{2,0},{3,1},{4,6},{5,7},{6,4},{7,5},{8,10},{9,11},{10,... | collective-permute-start | bytes 196616 | tf_op jit(solution)/shard_map/ppermute | solution.py:222
  108.1 4.6 %collective-permute-start.27 = (bf16[64,512]{1,0:T(8,128)(2,1)S(1)}, bf16[64,512]{1,0:T(8,128)(2,1)S(1)}, u32[]{:S(2)}, u32[]{:S(2)}) collective-permute-start(bf16[64,512]{1,0:T(8,128)(2,1)S(1)} %get-tuple-element.71), channel_id=1, source_target_pairs={{0,4},{1,5},{2,6},{3,7},{4,0},{5,1},{6,2},{7,3},{8,12},{9,13},{10,... | collective-permute-start | bytes 196616 | tf_op jit(solution)/shard_map/ppermute | solution.py:222
  109.6 5.9 %collective-permute-start.29 = (bf16[64,512]{1,0:T(8,128)(2,1)S(1)}, bf16[64,512]{1,0:T(8,128)(2,1)S(1)}, u32[]{:S(2)}, u32[]{:S(2)}) collective-permute-start(bf16[64,512]{1,0:T(8,128)(2,1)S(1)} %get-tuple-element.75), channel_id=1, source_target_pairs={{0,8},{1,9},{2,10},{3,11},{4,12},{5,13},{6,14},{7,15},{8,0},{9,1},... | collective-permute-start | bytes 196616 | tf_op jit(solution)/shard_map/ppermute | solution.py:222
  111.2 6.1 %collective-permute-start.30 = (bf16[64,512]{1,0:T(8,128)(2,1)S(1)}, bf16[64,512]{1,0:T(8,128)(2,1)S(1)}, u32[]{:S(2)}, u32[]{:S(2)}) collective-permute-start(bf16[64,512]{1,0:T(8,128)(2,1)S(1)} %get-tuple-element.76), channel_id=1, source_target_pairs={{0,12},{1,13},{2,14},{3,15},{4,8},{5,9},{6,10},{7,11},{8,4},{9,5},... | collective-permute-start | bytes 196616 | tf_op jit(solution)/shard_map/ppermute | solution.py:222
  (7 other events, 14.6 us)

commit v3 on v2

--- a/solution.py
+++ b/solution.py
@@ -11,6 +11,7 @@
 AXES = ("grp", "vec", "occ", "wlk")
 HALVES = 2
 LOADS = 4
+STREAMS = 4
 LARGE = pltpu.CompilerParams(vmem_limit_bytes=44 * 2**20)
 SMALL = pltpu.CompilerParams(vmem_limit_bytes=24 * 2**20)
 
@@ -46,21 +47,25 @@
     return moved % shards if isinstance(moved, int) else lax.rem(moved, shards)
 
 
-def load_body(first, source, out, arrived):
-    copy = pltpu.make_async_copy(source.at[pl.ds(first, out.shape[0])], out, arrived)
-    copy.start()
-    copy.wait()
-
-
-def loaded(factors, first, count):
+def load_body(first, place, source, out, arrived):
+    del place
+    rows = out.shape[0] // STREAMS
+    copies = [pltpu.make_async_copy(source.at[pl.ds(first + at * rows, rows)], out.at[pl.ds(at * rows, rows)], arrived.at[at]) for at in range(STREAMS)]
+    for copy in copies:
+        copy.start()
+    for copy in copies:
+        copy.wait()
+
+
+def loaded(place, factors, first, count):
     return pl.pallas_call(
         functools.partial(load_body, first),
-        in_specs=[pl.BlockSpec(memory_space=pltpu.HBM)],
+        in_specs=[SMEM, pl.BlockSpec(memory_space=pltpu.HBM)],
         out_specs=VMEM,
         out_shape=pltpu.VMEM((count, factors.shape[1]), factors.dtype),
-        scratch_shapes=[pltpu.SemaphoreType.DMA],
+        scratch_shapes=[pltpu.SemaphoreType.DMA((STREAMS,))],
         compiler_params=LARGE,
-    )(factors)
+    )(place, factors)
 
 
 def amplitude_body(shards, loads, half, place, *refs):
@@ -97,19 +102,27 @@
     )(place, *factors, *pieces)
 
 
-def gradient_body(shards, loads, groups, place, own, far, *refs):
-    factors, outs, sums = refs[:loads], refs[loads:-1], refs[-1]
-    width = own.shape[1]
-    part, at = width // HALVES, 0
+def gradient_body(shards, counts, carried, groups, place, *refs):
+    owns, fars, factors = refs[: counts[0]], refs[counts[0] : 2 * counts[0]], refs[2 * counts[0] : 2 * counts[0] + counts[1]]
+    outs, sums = refs[2 * counts[0] + counts[1] + carried : -1], refs[-1]
+    width = owns[0].shape[1]
+    part = width // HALVES
+    slots = [(at, g) for at, own in enumerate(owns) for g in range(own.shape[0] // part)]
+    seen = 0
     for chunk in factors:
-        vectors = range(at, at + chunk.shape[0] // width)
-        wide = [jnp.concatenate([side[g * part : (g + 1) * part, :] for g in vectors], axis=1) for side in (own, far)]
+        vectors = slots[seen : seen + chunk.shape[0] // width]
+        wide = [jnp.concatenate([side[at][g * part : (g + 1) * part, :] for at, g in vectors], axis=1) for side in (owns, fars)]
         grown = jnp.dot(jnp.concatenate(wide, axis=0), chunk[...], preferred_element_type=jnp.float32)
-        if at == 0:
+        if seen == 0 and carried:
+            sums[...] = refs[2 * counts[0] + counts[1]][...] + grown
+        elif seen == 0:
             sums[...] = grown
         else:
             sums[...] += grown
-        at += len(vectors)
+        seen += len(vectors)
+    if len(outs) == 1:
+        outs[0][...] = sums[...]
+        return
     owned = sums.shape[1] // shards
     for hop in range(shards):
         low = pl.multiple_of(peer(place[0], hop, shards) * owned, owned)
@@ -123,39 +136,46 @@
                 outs[shards + group][:, to : to + owned] = sums[part:, pl.ds(low, owned)].astype(jnp.bfloat16)
 
 
-def gradients_of(place, factors, own, far, shards, groups=None):
-    orbitals, width = factors[0].shape[1], own.shape[1]
+def gradients_of(place, factors, owns, fars, shards, groups=None, carried=None, more=False):
+    orbitals, width = factors[0].shape[1], owns[0].shape[1]
     part, owned = width // HALVES, orbitals // shards
-    rows = part if groups else 2 * part
-    outs = [jax.ShapeDtypeStruct((rows, owned), jnp.bfloat16 if hop else jnp.float32) for hop in range(shards)]
-    if groups:
+    outs = [jax.ShapeDtypeStruct((2 * part, owned), jnp.bfloat16 if hop else jnp.float32) for hop in range(shards)]
+    if more:
+        outs = [jax.ShapeDtypeStruct((2 * part, orbitals), jnp.float32)]
+    elif groups:
         outs = [jax.ShapeDtypeStruct((part, owned), jnp.float32)] * shards
         outs += [jax.ShapeDtypeStruct((part, owned * len(hops)), jnp.bfloat16) for hops in groups]
     count = sum(chunk.shape[0] for chunk in factors)
+    values = [place, *owns, *fars, *factors] + ([] if carried is None else [carried])
     return pl.pallas_call(
-        functools.partial(gradient_body, shards, len(factors), groups),
-        in_specs=[SMEM] + [VMEM] * (2 + len(factors)),
+        functools.partial(gradient_body, shards, (len(owns), len(factors)), 0 if carried is None else 1, groups),
+        in_specs=[SMEM] + [VMEM] * (len(values) - 1),
         out_specs=[VMEM] * len(outs),
         scratch_shapes=[pltpu.VMEM((2 * part, orbitals), jnp.float32)],
         out_shape=outs,
         compiler_params=SMALL,
         cost_estimate=pl.CostEstimate(flops=4 * count * orbitals * part, transcendentals=0, bytes_accessed=2 * count * orbitals),
-    )(place, own, far, *factors)
-
-
-def split_body(*refs):
-    total = refs[0][...].astype(jnp.float32)
-    for part in refs[1:-2]:
-        total = total + part[...].astype(jnp.float32)
-    half = total.shape[0] // 2
-    refs[-2][...] = total[:half]
-    refs[-1][...] = total[half:].astype(jnp.bfloat16)
-
-
-def split_sum(parts):
-    rows, columns = parts[0].shape
-    outs = [jax.ShapeDtypeStruct((rows // 2, columns), kind) for kind in (jnp.float32, jnp.bfloat16)]
-    return pl.pallas_call(split_body, out_shape=outs, compiler_params=SMALL)(*parts)
+    )(*values)
+
+
+def split_body(each, *refs):
+    inputs, outs = refs[: -(len(refs) // (each + 1)) - 1], refs[-(len(refs) // (each + 1)) - 1 :]
+    for stage, own in enumerate(outs[:-1]):
+        parts = inputs[stage * each : (stage + 1) * each]
+        total = parts[0][...].astype(jnp.float32)
+        for part in parts[1:]:
+            total = total + part[...].astype(jnp.float32)
+        half = own.shape[0]
+        own[...] = total[:half]
+        outs[-1][stage * half : (stage + 1) * half, :] = total[half:].astype(jnp.bfloat16)
+
+
+def split_sums(stages):
+    rows, columns = stages[0][0].shape
+    outs = [jax.ShapeDtypeStruct((rows // 2, columns), jnp.float32)] * len(stages)
+    outs += [jax.ShapeDtypeStruct((len(stages) * (rows // 2), columns), jnp.bfloat16)]
+    flat = [part for stage in stages for part in stage]
+    return pl.pallas_call(functools.partial(split_body, len(stages[0])), out_shape=outs, compiler_params=SMALL)(*flat)
 
 
 def join_body(came, *refs):
@@ -171,26 +191,34 @@
     return pl.pallas_call(join_body, out_shape=outs, compiler_params=SMALL)(came, *owns)
 
 
-def total_body(counts, *refs):
-    out, at = refs[-1], 0
-    for walker, halves in enumerate(counts):
+def total_body(plan, *refs):
+    out = refs[-1]
+    for walker, halves in enumerate(plan):
         rows = []
-        for count in halves:
-            total = refs[at][...].astype(jnp.float32)
-            for part in refs[at + 1 : at + count]:
-                total = total + part[...].astype(jnp.float32)
+        for parts in halves:
+            total = None
+            for at, low, high in parts:
+                value = refs[at][low:high, :].astype(jnp.float32)
+                total = value if total is None else total + value
             rows.append(total)
-            at += count
         out[walker] = -jnp.concatenate(rows, axis=0).T
 
 
-def totals_of(pieces):
-    part, owned = pieces[0][0][0].shape
+def totals_of(values, plan):
+    part, owned = values[0].shape
     return pl.pallas_call(
-        functools.partial(total_body, [[len(half) for half in walker] for walker in pieces]),
-        out_shape=jax.ShapeDtypeStruct((len(pieces), owned, part * HALVES), jnp.float32),
+        functools.partial(total_body, plan),
+        out_shape=jax.ShapeDtypeStruct((len(plan), owned, part * HALVES), jnp.float32),
         compiler_params=SMALL,
-    )(*[piece for walker in pieces for half in walker for piece in half])
+    )(*values)
+
+
+def parts_of(stage, stages):
+    if stage == 0:
+        return [[0], list(range(1, LOADS))]
+    if stage == stages - 1:
+        return [list(range(LOADS - 1)), [LOADS - 1]]
+    return [list(range(LOADS))]
 
 
 def paired(shape, chol_half, theta):
@@ -204,9 +232,10 @@
     position = lax.axis_index("vec")
     place = position.reshape(1)
     whole = chol_half.reshape(vectors * width, orbitals)
+    rows = vectors // LOADS * width
     factors = []
     for load in range(LOADS):
-        factors.append(loaded(whole, load * vectors // LOADS * width, vectors // LOADS * width))
+        factors.append(loaded(place, whole, load * rows, rows))
 
     def flat(grp, vec, occ, wlk):
         return ((grp * shape["vec"] + vec) * shape["occ"] + occ) * shape["wlk"] + wlk
@@ -234,23 +263,35 @@
     groups = [list(range(half)), list(range(half, shards))]
     sides = []
     for stage in range(stages):
-        own, far = amplitudes_of(place, factors, blocks[stage // HALVES], stage % HALVES, width, shards)
-        sides.append([own, moved(far, 0, True)])
-
-    pieces = [[] for _ in range(walkers)]
-    for stage in range(stages):
-        got = gradients_of(place, factors, *sides[stage], shards, groups if stage == stages - 1 else None)
-        if stage < stages - 1:
-            arrived = [got[0]] + [moved(got[hop], hop) for hop in hops]
-            own, far = split_sum(arrived)
-            pieces[stage // HALVES].append([own, moved(far, 0, True)])
-        else:
-            came = [moved(got[shards + at], 0, True) for at in range(len(groups))]
-            owned = []
-            for at, hops_of in enumerate(groups):
-                owned += join_sums(came[at], [got[hop] for hop in hops_of], [jnp.bfloat16 if hop else jnp.float32 for hop in hops_of])
-            pieces[stage // HALVES].append([owned[0]] + [moved(owned[hop], hop) for hop in hops])
-    return totals_of(pieces)
+        owns, fars = [], []
+        for loads in parts_of(stage, stages):
+            own, far = amplitudes_of(place, [factors[load] for load in loads], blocks[stage // HALVES], stage % HALVES, width, shards)
+            owns.append(own)
+            fars.append(moved(far, 0, True))
+        sides.append((owns, fars))
+
+    arrived = []
+    for stage in range(stages - 1):
+        got = gradients_of(place, factors, *sides[stage], shards)
+        arrived.append([got[0]] + [moved(got[hop], hop) for hop in hops])
+
+    owns, fars = sides[-1]
+    first, then = parts_of(stages - 1, stages)
+    (carried,) = gradients_of(place, [factors[load] for load in first], owns[:1], fars[:1], shards, more=True)
+    got = gradients_of(place, [factors[load] for load in then], owns[1:], fars[1:], shards, groups, carried)
+    came = [moved(got[shards + at], 0, True) for at in range(len(groups))]
+    *kept, crossing = split_sums(arrived)
+    crossed = moved(crossing, 0, True)
+    owned = []
+    for at, hops_of in enumerate(groups):
+        owned += join_sums(came[at], [got[hop] for hop in hops_of], [jnp.bfloat16 if hop else jnp.float32 for hop in hops_of])
+    ends = [owned[0]] + [moved(owned[hop], hop) for hop in hops]
+
+    part = width // HALVES
+    values = [*kept, crossed, *ends]
+    plan = [[(stage, 0, part), (stages - 1, stage * part, (stage + 1) * part)] for stage in range(stages - 1)]
+    plan.append([(stages + at, 0, part) for at in range(len(ends))])
+    return totals_of(values, [plan[walker * HALVES : (walker + 1) * HALVES] for walker in range(walkers)])
 
 
 def solution(mesh):

time: 119 us -> 113 us (0.950)
  local copies, waits for them, and re-layouts: 17.7 us -> 1.01 us
  waiting for transfers between devices: 25.5 us -> 36.9 us
    unnamed x16 -> x0, local copies, waits for them, and re-layouts: 16.7 us -> none
    ppermute x31, waiting for transfers between devices: 25.5 us -> 36.9 us  [moved(): return lax.ppermute(value, AXES, pairs)]
    pallas_call x4 -> x6, Pallas kernels: 9.83 us -> 10.5 us  [amplitudes_of(): pl.pallas_call(functools.partial(amplitude_body, shards, len(factors), ha...]
    pallas_call x12 -> x11, Pallas kernels: 20.1 us -> 20 us  [the longest x5 9.99 us: gradients_of(): pl.pallas_call(functools.partial(gradient_body, shards, (len(owns), len(f...]
  transfers between devices with their start and end apart: 31 -> 31, of which waited for: 8 -> 9; matrix products, arithmetic and copies ran while one was open for 1% -> 1% of each run, Pallas kernels for 24% -> 26%
where the time goes in v3:
time: 113 us
  starting transfers between devices  43.9 us (39%)
  waiting for transfers between devices  36.9 us (33%)
  Pallas kernels  30.5 us (27%)
    ppermute x31, starting transfers between devices, moved(): return lax.ppermute(value, AXES, pairs)  43.9 us
    ppermute x31, waiting for transfers between devices, moved(): return lax.ppermute(value, AXES, pairs)  36.9 us
    pallas_call x6, Pallas kernels, amplitudes_of(): pl.pallas_call(functools.partial(amplitude_body, shards, len(factors), ha...  10.5 us
    pallas_call x5, Pallas kernels, gradients_of(): pl.pallas_call(functools.partial(gradient_body, shards, (len(owns), len(f...  9.99 us
    pallas_call x4, Pallas kernels, loaded(): pl.pallas_call(functools.partial(load_body, first), in_specs=[SMEM, pl.Bl...  8.83 us
  transfers between devices with their start and end apart: 31, of which 9 were waited for; matrix products, arithmetic and copies ran while one was open for 1% of the time, Pallas kernels for 26%

profile of v3, /device:TPU:0, one launch (start us, length us, event | category | flops | bytes accessed | tf_op | source)
XLA Modules:
  0.0 112.5 jit_solution(10449632498237042675)
XLA Ops:
  0.0 3.0 %collective-permute-start.3 = (bf16[2,512,128]{2,1,0:T(8,128)(2,1)}, bf16[2,512,128]{2,1,0:T(8,128)(2,1)S(1)}, u32[]{:S(2)}, u32[]{:S(2)}) collective-permute-start(bf16[2,512,128]{2,1,0:T(8,128)(2,1)} %param.3), channel_id=1, source_target_pairs={{0,2},{1,3},{2,0},{3,1},{4,6},{5,7},{6,4},{7,5},{8,10},{9,11},{10,... | collective-permute-start | bytes 786440 | tf_op jit(solution)/shard_map/ppermute | solution.py:251
  4.0 1.6 %collective-permute-start = (bf16[512,128]{1,0:T(8,128)(2,1)S(1)}, bf16[512,128]{1,0:T(8,128)(2,1)S(1)}, u32[]{:S(2)}, u32[]{:S(2)}) collective-permute-start(bf16[512,128]{1,0:T(8,128)(2,1)S(1)} %get-tuple-element.82.refs_1_.refs_3_.refs_4_), channel_id=1, source_target_pairs={{0,4},{1,5},{2,6},{3,7},{4,0},{5,1},{6,2},{7,3},{8,12},{9,13},{10,... | collective-permute-start | bytes 393224 | tf_op jit(solution)/shard_map/ppermute | solution.py:251
  5.6 2.6 %collective-permute-start.1 = (bf16[512,128]{1,0:T(8,128)(2,1)S(1)}, bf16[512,128]{1,0:T(8,128)(2,1)S(1)}, u32[]{:S(2)}, u32[]{:S(2)}) collective-permute-start(bf16[512,128]{1,0:T(8,128)(2,1)S(1)} %get-tuple-element.82.refs_1_.refs_3_.refs_4_), channel_id=1, source_target_pairs={{0,8},{1,9},{2,10},{3,11},{4,12},{5,13},{6,14},{7,15},{8,0},{9,1},... | collective-permute-start | bytes 393224 | tf_op jit(solution)/shard_map/ppermute | solution.py:251
  8.4 2.2 %shard_map.28.refs_0_.refs_4_.refs_2_ = bf16[1024,2048]{1,0:T(8,128)(2,1)S(1)} custom-call(s32[1]{0:T(128)} %bitcast.place, bf16[4096,2048]{1,0:T(8,128)(2,1)} %bitcast.10), custom_call_target="tpu_custom_call" | custom-call | tf_op jit(solution)/shard_map/pallas_call | solution.py:61
  10.6 2.2 %shard_map.30.refs_0_.refs_5_.refs_1_.refs_3_ = bf16[1024,2048]{1,0:T(8,128)(2,1)S(1)} custom-call(s32[1]{0:T(128)} %bitcast.place, bf16[4096,2048]{1,0:T(8,128)(2,1)} %bitcast.11), custom_call_target="tpu_custom_call" | custom-call | tf_op jit(solution)/shard_map/pallas_call | solution.py:61
  12.8 2.2 %shard_map.31.refs_1_.refs_6_.refs_2_.refs_4_ = bf16[1024,2048]{1,0:T(8,128)(2,1)S(1)} custom-call(s32[1]{0:T(128)} %bitcast.place, bf16[4096,2048]{1,0:T(8,128)(2,1)} %bitcast.12), custom_call_target="tpu_custom_call" | custom-call | tf_op jit(solution)/shard_map/pallas_call | solution.py:61
  15.1 2.2 %shard_map.32.refs_2_.refs_7_.refs_3_.refs_5_.refs_0_ = bf16[1024,2048]{1,0:T(8,128)(2,1)S(1)} custom-call(s32[1]{0:T(128)} %bitcast.place, bf16[4096,2048]{1,0:T(8,128)(2,1)} %bitcast.13), custom_call_target="tpu_custom_call" | custom-call | tf_op jit(solution)/shard_map/pallas_call | solution.py:61
  20.9 3.3 %collective-permute-start.17 = (bf16[512,256]{1,0:T(8,128)(2,1)S(1)}, bf16[512,256]{1,0:T(8,128)(2,1)S(1)}, u32[]{:S(2)}, u32[]{:S(2)}) collective-permute-start(bf16[512,256]{1,0:T(8,128)(2,1)S(1)} %pad_maximum_fusion.refs_4_.refs_1_.refs_3_), channel_id=1, source_target_pairs={{0,8},{1,9},{2,10},{3,11},{4,12},{5,13},{6,14},{7,15},{8,0},{9,1},... | collective-permute-start | bytes 786440 | tf_op jit(solution)/shard_map/ppermute | solution.py:251
  24.2 3.1 %collective-permute-start.18 = (bf16[512,256]{1,0:T(8,128)(2,1)S(1)}, bf16[512,256]{1,0:T(8,128)(2,1)S(1)}, u32[]{:S(2)}, u32[]{:S(2)}) collective-permute-start(bf16[512,256]{1,0:T(8,128)(2,1)S(1)} %pad_maximum_fusion.refs_4_.refs_1_.refs_3_), channel_id=1, source_target_pairs={{0,12},{1,13},{2,14},{3,15},{4,8},{5,9},{6,10},{7,11},{8,4},{9,5},... | collective-permute-start | bytes 786440 | tf_op jit(solution)/shard_map/ppermute | solution.py:251
  27.3 2.5 %shard_map.35 = (bf16[2048,128]{1,0:T(8,128)(2,1)S(1)}, bf16[2048,128]{1,0:T(8,128)(2,1)S(1)}) custom-call(s32[1]{0:T(128)} %bitcast.place, bf16[1024,2048]{1,0:T(8,128)(2,1)S(1)} %shard_map.28.refs_0_.refs_4_.refs_2_, bf16[1024,2048]{1,0:T(8,128)(2,1)S(1)} %shard_map.30.refs_0_.refs_5_.refs_1_.refs_3_, ...), custom_call_target="tpu_custom_call" | custom-call | flops 2147483648 | bytes 8388608 | tf_op jit(solution)/shard_map/pallas_call | solution.py:94
  30.5 2.0 %shard_map.33 = (bf16[1536,128]{1,0:T(8,128)(2,1)S(1)}, bf16[1536,128]{1,0:T(8,128)(2,1)S(1)}) custom-call(s32[1]{0:T(128)} %bitcast.place, bf16[1024,2048]{1,0:T(8,128)(2,1)S(1)} %shard_map.30.refs_0_.refs_5_.refs_1_.refs_3_, bf16[1024,2048]{1,0:T(8,128)(2,1)S(1)} %shard_map.31.refs_1_.refs_6_.refs_2_.refs_4_, ...), custom_call_target="tpu_custom_call" | custom-call | flops 1610612736 | bytes 6291456 | tf_op jit(solution)/shard_map/pallas_call | solution.py:94
  32.5 1.6 %collective-permute-start.8 = (bf16[1536,128]{1,0:T(8,128)(2,1)S(1)}, bf16[1536,128]{1,0:T(8,128)(2,1)S(1)}, u32[]{:S(2)}, u32[]{:S(2)}) collective-permute-start(bf16[1536,128]{1,0:T(8,128)(2,1)S(1)} %get-tuple-element.46), channel_id=1, source_target_pairs={{0,2},{1,3},{2,0},{3,1},{4,6},{5,7},{6,4},{7,5},{8,10},{9,11},{10,... | collective-permute-start | bytes 1179656 | tf_op jit(solution)/shard_map/ppermute | solution.py:251
  35.5 6.8 %collective-permute-done.17.refs_6_.refs_3_.refs_5_ = bf16[512,256]{1,0:T(8,128)(2,1)S(1)} collective-permute-done((bf16[512,256]{1,0:T(8,128)(2,1)S(1)}, bf16[512,256]{1,0:T(8,128)(2,1)S(1)}, u32[]{:S(2)}, u32[]{:S(2)}) %collective-permute-start.17) | collective-permute-done | bytes 262176 | tf_op jit(solution)/shard_map/ppermute | solution.py:251
  42.4 2.4 %shard_map.37 = (bf16[2048,128]{1,0:T(8,128)(2,1)S(1)}, bf16[2048,128]{1,0:T(8,128)(2,1)S(1)}) custom-call(s32[1]{0:T(128)} %bitcast.place, bf16[1024,2048]{1,0:T(8,128)(2,1)S(1)} %shard_map.28.refs_0_.refs_4_.refs_2_, bf16[1024,2048]{1,0:T(8,128)(2,1)S(1)} %shard_map.30.refs_0_.refs_5_.refs_1_.refs_3_, ...), custom_call_target="tpu_custom_call" | custom-call | flops 2147483648 | bytes 8388608 | tf_op jit(solution)/shard_map/pallas_call | solution.py:94
  44.8 1.6 %collective-permute-start.19 = (bf16[2048,128]{1,0:T(8,128)(2,1)S(1)}, bf16[2048,128]{1,0:T(8,128)(2,1)S(1)}, u32[]{:S(2)}, u32[]{:S(2)}) collective-permute-start(bf16[2048,128]{1,0:T(8,128)(2,1)S(1)} %get-tuple-element.58), channel_id=1, source_target_pairs={{0,2},{1,3},{2,0},{3,1},{4,6},{5,7},{6,4},{7,5},{8,10},{9,11},{10,... | collective-permute-start | bytes 1572872 | tf_op jit(solution)/shard_map/ppermute | solution.py:251
  46.4 1.9 %shard_map.41 = (bf16[1536,128]{1,0:T(8,128)(2,1)S(1)}, bf16[1536,128]{1,0:T(8,128)(2,1)S(1)}) custom-call(s32[1]{0:T(128)} %bitcast.place, bf16[1024,2048]{1,0:T(8,128)(2,1)S(1)} %shard_map.28.refs_0_.refs_4_.refs_2_, bf16[1024,2048]{1,0:T(8,128)(2,1)S(1)} %shard_map.30.refs_0_.refs_5_.refs_1_.refs_3_, ...), custom_call_target="tpu_custom_call" | custom-call | flops 1610612736 | bytes 6291456 | tf_op jit(solution)/shard_map/pallas_call | solution.py:94
  49.6 6.4 %collective-permute-done.7.refs_2_ = bf16[512,128]{1,0:T(8,128)(2,1)S(1)} collective-permute-done((bf16[512,128]{1,0:T(8,128)(2,1)S(1)}, bf16[512,128]{1,0:T(8,128)(2,1)S(1)}, u32[]{:S(2)}, u32[]{:S(2)}) %collective-permute-start.7) | collective-permute-done | bytes 131104 | tf_op jit(solution)/shard_map/ppermute | solution.py:251
  56.5 2.4 %shard_map.34 = (f32[128,512]{1,0:T(8,128)S(1)}, bf16[128,512]{1,0:T(8,128)(2,1)S(1)}, bf16[128,512]{1,0:T(8,128)(2,1)S(1)}, bf16[128,512]{1,0:T(8,128)(2,1)S(1)}) custom-call(s32[1]{0:T(128)} %bitcast.place, bf16[512,128]{1,0:T(8,128)(2,1)S(1)} %get-tuple-element.43.refs_0_, bf16[1536,128]{1,0:T(8,128)(2,1)S(1)} %get-tuple-element.44.refs_1_, ...), custom_call_target="tpu_custom_call" | custom-call | flops 2147483648 | bytes 16777216 | tf_op jit(solution)/shard_map/pallas_call | solution.py:150
  58.9 1.5 %collective-permute-start.10 = (bf16[128,512]{1,0:T(8,128)(2,1)S(1)}, bf16[128,512]{1,0:T(8,128)(2,1)S(1)}, u32[]{:S(2)}, u32[]{:S(2)}) collective-permute-start(bf16[128,512]{1,0:T(8,128)(2,1)S(1)} %get-tuple-element.49), channel_id=1, source_target_pairs={{0,8},{1,9},{2,10},{3,11},{4,12},{5,13},{6,14},{7,15},{8,0},{9,1},... | collective-permute-start | bytes 393224 | tf_op jit(solution)/shard_map/ppermute | solution.py:251
  60.4 2.0 %collective-permute-start.11 = (bf16[128,512]{1,0:T(8,128)(2,1)S(1)}, bf16[128,512]{1,0:T(8,128)(2,1)S(1)}, u32[]{:S(2)}, u32[]{:S(2)}) collective-permute-start(bf16[128,512]{1,0:T(8,128)(2,1)S(1)} %get-tuple-element.50), channel_id=1, source_target_pairs={{0,12},{1,13},{2,14},{3,15},{4,8},{5,9},{6,10},{7,11},{8,4},{9,5},... | collective-permute-start | bytes 393224 | tf_op jit(solution)/shard_map/ppermute | solution.py:251
  62.4 2.6 %shard_map.36 = (f32[128,512]{1,0:T(8,128)S(1)}, bf16[128,512]{1,0:T(8,128)(2,1)S(1)}, bf16[128,512]{1,0:T(8,128)(2,1)S(1)}, bf16[128,512]{1,0:T(8,128)(2,1)S(1)}) custom-call(s32[1]{0:T(128)} %bitcast.place, bf16[2048,128]{1,0:T(8,128)(2,1)S(1)} %get-tuple-element.51.refs_0_, bf16[2048,128]{1,0:T(8,128)(2,1)S(1)} %collective-permute-done.12.refs_1_, ...), custom_call_target="tpu_custom_call" | custom-call | flops 2147483648 | bytes 16777216 | tf_op jit(solution)/shard_map/pallas_call | solution.py:150
  65.0 10.2 %collective-permute-done.24.refs_1_ = bf16[512,128]{1,0:T(8,128)(2,1)S(1)} collective-permute-done((bf16[512,128]{1,0:T(8,128)(2,1)S(1)}, bf16[512,128]{1,0:T(8,128)(2,1)S(1)}, u32[]{:S(2)}, u32[]{:S(2)}) %collective-permute-start.24) | collective-permute-done | bytes 131104 | tf_op jit(solution)/shard_map/ppermute | solution.py:251
  77.2 2.4 %shard_map.38 = (f32[128,512]{1,0:T(8,128)S(1)}, bf16[128,512]{1,0:T(8,128)(2,1)S(1)}, bf16[128,512]{1,0:T(8,128)(2,1)S(1)}, bf16[128,512]{1,0:T(8,128)(2,1)S(1)}) custom-call(s32[1]{0:T(128)} %bitcast.place, bf16[2048,128]{1,0:T(8,128)(2,1)S(1)} %get-tuple-element.57.refs_0_, bf16[2048,128]{1,0:T(8,128)(2,1)S(1)} %collective-permute-done.19.refs_1_, ...), custom_call_target="tpu_custom_call" | custom-call | flops 2147483648 | bytes 16777216 | tf_op jit(solution)/shard_map/pallas_call | solution.py:150
  79.7 2.1 %collective-permute-start.14 = (bf16[128,512]{1,0:T(8,128)(2,1)S(1)}, bf16[128,512]{1,0:T(8,128)(2,1)S(1)}, u32[]{:S(2)}, u32[]{:S(2)}) collective-permute-start(bf16[128,512]{1,0:T(8,128)(2,1)S(1)} %get-tuple-element.55), channel_id=1, source_target_pairs={{0,8},{1,9},{2,10},{3,11},{4,12},{5,13},{6,14},{7,15},{8,0},{9,1},... | collective-permute-start | bytes 393224 | tf_op jit(solution)/shard_map/ppermute | solution.py:251
  81.8 1.5 %collective-permute-start.15 = (bf16[128,512]{1,0:T(8,128)(2,1)S(1)}, bf16[128,512]{1,0:T(8,128)(2,1)S(1)}, u32[]{:S(2)}, u32[]{:S(2)}) collective-permute-start(bf16[128,512]{1,0:T(8,128)(2,1)S(1)} %get-tuple-element.56), channel_id=1, source_target_pairs={{0,12},{1,13},{2,14},{3,15},{4,8},{5,9},{6,10},{7,11},{8,4},{9,5},... | collective-permute-start | bytes 393224 | tf_op jit(solution)/shard_map/ppermute | solution.py:251
  84.9 2.6 %collective-permute-start.21 = (bf16[128,512]{1,0:T(8,128)(2,1)S(1)}, bf16[128,512]{1,0:T(8,128)(2,1)S(1)}, u32[]{:S(2)}, u32[]{:S(2)}) collective-permute-start(bf16[128,512]{1,0:T(8,128)(2,1)S(1)} %get-tuple-element.61), channel_id=1, source_target_pairs={{0,8},{1,9},{2,10},{3,11},{4,12},{5,13},{6,14},{7,15},{8,0},{9,1},... | collective-permute-start | bytes 393224 | tf_op jit(solution)/shard_map/ppermute | solution.py:251
  87.5 2.1 %collective-permute-start.22 = (bf16[128,512]{1,0:T(8,128)(2,1)S(1)}, bf16[128,512]{1,0:T(8,128)(2,1)S(1)}, u32[]{:S(2)}, u32[]{:S(2)}) collective-permute-start(bf16[128,512]{1,0:T(8,128)(2,1)S(1)} %get-tuple-element.62), channel_id=1, source_target_pairs={{0,12},{1,13},{2,14},{3,15},{4,8},{5,9},{6,10},{7,11},{8,4},{9,5},... | collective-permute-start | bytes 393224 | tf_op jit(solution)/shard_map/ppermute | solution.py:251
  89.6 1.8 %shard_map.42.refs_3_ = f32[128,2048]{1,0:T(8,128)S(1)} custom-call(s32[1]{0:T(128)} %bitcast.place, bf16[1536,128]{1,0:T(8,128)(2,1)S(1)} %get-tuple-element.69.refs_0_, bf16[1536,128]{1,0:T(8,128)(2,1)S(1)} %collective-permute-done.25.refs_1_, bf16[1024,2048]{1,0:T(8,128)(2,1)S(1)} %shard_map.28.refs_0_.refs_4_.refs_2_, ...), custom_call_target="tpu_custom_call" | custom-call | flops 1610612736 | bytes 12582912 | tf_op jit(solution)/shard_map/pallas_call | solution.py:150
  94.6 6.3 %collective-permute-done.21.refs_10_ = bf16[128,512]{1,0:T(8,128)(2,1)S(1)} collective-permute-done((bf16[128,512]{1,0:T(8,128)(2,1)S(1)}, bf16[128,512]{1,0:T(8,128)(2,1)S(1)}, u32[]{:S(2)}, u32[]{:S(2)}) %collective-permute-start.21) | collective-permute-done | bytes 131104 | tf_op jit(solution)/shard_map/ppermute | solution.py:251
  101.9 3.6 %collective-permute-start.29 = (bf16[64,512]{1,0:T(8,128)(2,1)S(1)}, bf16[64,512]{1,0:T(8,128)(2,1)S(1)}, u32[]{:S(2)}, u32[]{:S(2)}) collective-permute-start(bf16[64,512]{1,0:T(8,128)(2,1)S(1)} %get-tuple-element.79), channel_id=1, source_target_pairs={{0,8},{1,9},{2,10},{3,11},{4,12},{5,13},{6,14},{7,15},{8,0},{9,1},... | collective-permute-start | bytes 196616 | tf_op jit(solution)/shard_map/ppermute | solution.py:251
  106.4 2.6 %collective-permute-done.29.refs_6_ = bf16[64,512]{1,0:T(8,128)(2,1)S(1)} collective-permute-done((bf16[64,512]{1,0:T(8,128)(2,1)S(1)}, bf16[64,512]{1,0:T(8,128)(2,1)S(1)}, u32[]{:S(2)}, u32[]{:S(2)}) %collective-permute-start.29) | collective-permute-done | bytes 65568 | tf_op jit(solution)/shard_map/ppermute | solution.py:251
  109.0 2.5 %collective-permute-done.30.refs_7_ = bf16[64,512]{1,0:T(8,128)(2,1)S(1)} collective-permute-done((bf16[64,512]{1,0:T(8,128)(2,1)S(1)}, bf16[64,512]{1,0:T(8,128)(2,1)S(1)}, u32[]{:S(2)}, u32[]{:S(2)}) %collective-permute-start.30) | collective-permute-done | bytes 65568 | tf_op jit(solution)/shard_map/ppermute | solution.py:251
  (52 shorter events, 18.5 us)
Async XLA Ops:
  0.0 20.3 %collective-permute-start.3 = (bf16[2,512,128]{2,1,0:T(8,128)(2,1)}, bf16[2,512,128]{2,1,0:T(8,128)(2,1)S(1)}, u32[]{:S(2)}, u32[]{:S(2)}) collective-permute-start(bf16[2,512,128]{2,1,0:T(8,128)(2,1)} %param.3), channel_id=1, source_target_pairs={{0,2},{1,3},{2,0},{3,1},{4,6},{5,7},{6,4},{7,5},{8,10},{9,11},{10,... | collective-permute-start | bytes 786440 | tf_op jit(solution)/shard_map/ppermute | solution.py:251
  4.0 13.3 %collective-permute-start = (bf16[512,128]{1,0:T(8,128)(2,1)S(1)}, bf16[512,128]{1,0:T(8,128)(2,1)S(1)}, u32[]{:S(2)}, u32[]{:S(2)}) collective-permute-start(bf16[512,128]{1,0:T(8,128)(2,1)S(1)} %get-tuple-element.82.refs_1_.refs_3_.refs_4_), channel_id=1, source_target_pairs={{0,4},{1,5},{2,6},{3,7},{4,0},{5,1},{6,2},{7,3},{8,12},{9,13},{10,... | collective-permute-start | bytes 393224 | tf_op jit(solution)/shard_map/ppermute | solution.py:251
  5.6 12.6 %collective-permute-start.1 = (bf16[512,128]{1,0:T(8,128)(2,1)S(1)}, bf16[512,128]{1,0:T(8,128)(2,1)S(1)}, u32[]{:S(2)}, u32[]{:S(2)}) collective-permute-start(bf16[512,128]{1,0:T(8,128)(2,1)S(1)} %get-tuple-element.82.refs_1_.refs_3_.refs_4_), channel_id=1, source_target_pairs={{0,8},{1,9},{2,10},{3,11},{4,12},{5,13},{6,14},{7,15},{8,0},{9,1},... | collective-permute-start | bytes 393224 | tf_op jit(solution)/shard_map/ppermute | solution.py:251
  8.2 11.2 %collective-permute-start.2 = (bf16[512,128]{1,0:T(8,128)(2,1)S(1)}, bf16[512,128]{1,0:T(8,128)(2,1)S(1)}, u32[]{:S(2)}, u32[]{:S(2)}) collective-permute-start(bf16[512,128]{1,0:T(8,128)(2,1)S(1)} %get-tuple-element.82.refs_1_.refs_3_.refs_4_), channel_id=1, source_target_pairs={{0,12},{1,13},{2,14},{3,15},{4,8},{5,9},{6,10},{7,11},{8,4},{9,5},... | collective-permute-start | bytes 393224 | tf_op jit(solution)/shard_map/ppermute | solution.py:251
  17.3 6.9 %collective-permute-start.4 = (bf16[512,128]{1,0:T(8,128)(2,1)S(1)}, bf16[512,128]{1,0:T(8,128)(2,1)S(1)}, u32[]{:S(2)}, u32[]{:S(2)}) collective-permute-start(bf16[512,128]{1,0:T(8,128)(2,1)S(1)} %collective-permute-done.refs_2_.refs_4_.refs_5_), channel_id=1, source_target_pairs={{0,2},{1,3},{2,0},{3,1},{4,6},{5,7},{6,4},{7,5},{8,10},{9,11},{10,... | collective-permute-start | bytes 393224 | tf_op jit(solution)/shard_map/ppermute | solution.py:251
  18.3 9.1 %collective-permute-start.5 = (bf16[512,128]{1,0:T(8,128)(2,1)S(1)}, bf16[512,128]{1,0:T(8,128)(2,1)S(1)}, u32[]{:S(2)}, u32[]{:S(2)}) collective-permute-start(bf16[512,128]{1,0:T(8,128)(2,1)S(1)} %collective-permute-done.1.refs_3_.refs_5_.refs_6_), channel_id=1, source_target_pairs={{0,2},{1,3},{2,0},{3,1},{4,6},{5,7},{6,4},{7,5},{8,10},{9,11},{10,... | collective-permute-start | bytes 393224 | tf_op jit(solution)/shard_map/ppermute | solution.py:251
  19.4 7.9 %collective-permute-start.6 = (bf16[512,128]{1,0:T(8,128)(2,1)S(1)}, bf16[512,128]{1,0:T(8,128)(2,1)S(1)}, u32[]{:S(2)}, u32[]{:S(2)}) collective-permute-start(bf16[512,128]{1,0:T(8,128)(2,1)S(1)} %collective-permute-done.2.refs_4_.refs_6_.refs_7_), channel_id=1, source_target_pairs={{0,2},{1,3},{2,0},{3,1},{4,6},{5,7},{6,4},{7,5},{8,10},{9,11},{10,... | collective-permute-start | bytes 393224 | tf_op jit(solution)/shard_map/ppermute | solution.py:251
  20.4 14.6 %collective-permute-start.16 = (bf16[512,256]{1,0:T(8,128)(2,1)S(1)}, bf16[512,256]{1,0:T(8,128)(2,1)S(1)}, u32[]{:S(2)}, u32[]{:S(2)}) collective-permute-start(bf16[512,256]{1,0:T(8,128)(2,1)S(1)} %pad_maximum_fusion.refs_4_.refs_1_.refs_3_), channel_id=1, source_target_pairs={{0,4},{1,5},{2,6},{3,7},{4,0},{5,1},{6,2},{7,3},{8,12},{9,13},{10,... | collective-permute-start | bytes 786440 | tf_op jit(solution)/shard_map/ppermute | solution.py:251
  20.9 21.5 %collective-permute-start.17 = (bf16[512,256]{1,0:T(8,128)(2,1)S(1)}, bf16[512,256]{1,0:T(8,128)(2,1)S(1)}, u32[]{:S(2)}, u32[]{:S(2)}) collective-permute-start(bf16[512,256]{1,0:T(8,128)(2,1)S(1)} %pad_maximum_fusion.refs_4_.refs_1_.refs_3_), channel_id=1, source_target_pairs={{0,8},{1,9},{2,10},{3,11},{4,12},{5,13},{6,14},{7,15},{8,0},{9,1},... | collective-permute-start | bytes 786440 | tf_op jit(solution)/shard_map/ppermute | solution.py:251
  24.2 18.2 %collective-permute-start.18 = (bf16[512,256]{1,0:T(8,128)(2,1)S(1)}, bf16[512,256]{1,0:T(8,128)(2,1)S(1)}, u32[]{:S(2)}, u32[]{:S(2)}) collective-permute-start(bf16[512,256]{1,0:T(8,128)(2,1)S(1)} %pad_maximum_fusion.refs_4_.refs_1_.refs_3_), channel_id=1, source_target_pairs={{0,12},{1,13},{2,14},{3,15},{4,8},{5,9},{6,10},{7,11},{8,4},{9,5},... | collective-permute-start | bytes 786440 | tf_op jit(solution)/shard_map/ppermute | solution.py:251
  29.9 30.5 %collective-permute-start.12 = (bf16[2048,128]{1,0:T(8,128)(2,1)S(1)}, bf16[2048,128]{1,0:T(8,128)(2,1)S(1)}, u32[]{:S(2)}, u32[]{:S(2)}) collective-permute-start(bf16[2048,128]{1,0:T(8,128)(2,1)S(1)} %get-tuple-element.52), channel_id=1, source_target_pairs={{0,2},{1,3},{2,0},{3,1},{4,6},{5,7},{6,4},{7,5},{8,10},{9,11},{10,... | collective-permute-start | bytes 1572872 | tf_op jit(solution)/shard_map/ppermute | solution.py:251
  32.5 24.0 %collective-permute-start.8 = (bf16[1536,128]{1,0:T(8,128)(2,1)S(1)}, bf16[1536,128]{1,0:T(8,128)(2,1)S(1)}, u32[]{:S(2)}, u32[]{:S(2)}) collective-permute-start(bf16[1536,128]{1,0:T(8,128)(2,1)S(1)} %get-tuple-element.46), channel_id=1, source_target_pairs={{0,2},{1,3},{2,0},{3,1},{4,6},{5,7},{6,4},{7,5},{8,10},{9,11},{10,... | collective-permute-start | bytes 1179656 | tf_op jit(solution)/shard_map/ppermute | solution.py:251
  34.9 21.0 %collective-permute-start.7 = (bf16[512,128]{1,0:T(8,128)(2,1)S(1)}, bf16[512,128]{1,0:T(8,128)(2,1)S(1)}, u32[]{:S(2)}, u32[]{:S(2)}) collective-permute-start(bf16[512,128]{1,0:T(8,128)(2,1)S(1)} %get-tuple-element.45), channel_id=1, source_target_pairs={{0,2},{1,3},{2,0},{3,1},{4,6},{5,7},{6,4},{7,5},{8,10},{9,11},{10,... | collective-permute-start | bytes 393224 | tf_op jit(solution)/shard_map/ppermute | solution.py:251
  44.8 31.0 %collective-permute-start.19 = (bf16[2048,128]{1,0:T(8,128)(2,1)S(1)}, bf16[2048,128]{1,0:T(8,128)(2,1)S(1)}, u32[]{:S(2)}, u32[]{:S(2)}) collective-permute-start(bf16[2048,128]{1,0:T(8,128)(2,1)S(1)} %get-tuple-element.58), channel_id=1, source_target_pairs={{0,2},{1,3},{2,0},{3,1},{4,6},{5,7},{6,4},{7,5},{8,10},{9,11},{10,... | collective-permute-start | bytes 1572872 | tf_op jit(solution)/shard_map/ppermute | solution.py:251
  48.2 39.3 %collective-permute-start.25 = (bf16[1536,128]{1,0:T(8,128)(2,1)S(1)}, bf16[1536,128]{1,0:T(8,128)(2,1)S(1)}, u32[]{:S(2)}, u32[]{:S(2)}) collective-permute-start(bf16[1536,128]{1,0:T(8,128)(2,1)S(1)} %get-tuple-element.70), channel_id=1, source_target_pairs={{0,2},{1,3},{2,0},{3,1},{4,6},{5,7},{6,4},{7,5},{8,10},{9,11},{10,... | collective-permute-start | bytes 1179656 | tf_op jit(solution)/shard_map/ppermute | solution.py:251
  56.0 19.2 %collective-permute-start.24 = (bf16[512,128]{1,0:T(8,128)(2,1)S(1)}, bf16[512,128]{1,0:T(8,128)(2,1)S(1)}, u32[]{:S(2)}, u32[]{:S(2)}) collective-permute-start(bf16[512,128]{1,0:T(8,128)(2,1)S(1)} %get-tuple-element.68), channel_id=1, source_target_pairs={{0,2},{1,3},{2,0},{3,1},{4,6},{5,7},{6,4},{7,5},{8,10},{9,11},{10,... | collective-permute-start | bytes 393224 | tf_op jit(solution)/shard_map/ppermute | solution.py:251
  58.9 20.7 %collective-permute-start.10 = (bf16[128,512]{1,0:T(8,128)(2,1)S(1)}, bf16[128,512]{1,0:T(8,128)(2,1)S(1)}, u32[]{:S(2)}, u32[]{:S(2)}) collective-permute-start(bf16[128,512]{1,0:T(8,128)(2,1)S(1)} %get-tuple-element.49), channel_id=1, source_target_pairs={{0,8},{1,9},{2,10},{3,11},{4,12},{5,13},{6,14},{7,15},{8,0},{9,1},... | collective-permute-start | bytes 393224 | tf_op jit(solution)/shard_map/ppermute | solution.py:251
  60.4 21.3 %collective-permute-start.11 = (bf16[128,512]{1,0:T(8,128)(2,1)S(1)}, bf16[128,512]{1,0:T(8,128)(2,1)S(1)}, u32[]{:S(2)}, u32[]{:S(2)}) collective-permute-start(bf16[128,512]{1,0:T(8,128)(2,1)S(1)} %get-tuple-element.50), channel_id=1, source_target_pairs={{0,12},{1,13},{2,14},{3,15},{4,8},{5,9},{6,10},{7,11},{8,4},{9,5},... | collective-permute-start | bytes 393224 | tf_op jit(solution)/shard_map/ppermute | solution.py:251
  75.2 8.1 %collective-permute-start.9 = (bf16[128,512]{1,0:T(8,128)(2,1)S(1)}, bf16[128,512]{1,0:T(8,128)(2,1)S(1)}, u32[]{:S(2)}, u32[]{:S(2)}) collective-permute-start(bf16[128,512]{1,0:T(8,128)(2,1)S(1)} %get-tuple-element.48), channel_id=1, source_target_pairs={{0,4},{1,5},{2,6},{3,7},{4,0},{5,1},{6,2},{7,3},{8,12},{9,13},{10,... | collective-permute-start | bytes 393224 | tf_op jit(solution)/shard_map/ppermute | solution.py:251
  75.8 9.1 %collective-permute-start.13 = (bf16[128,512]{1,0:T(8,128)(2,1)S(1)}, bf16[128,512]{1,0:T(8,128)(2,1)S(1)}, u32[]{:S(2)}, u32[]{:S(2)}) collective-permute-start(bf16[128,512]{1,0:T(8,128)(2,1)S(1)} %get-tuple-element.54), channel_id=1, source_target_pairs={{0,4},{1,5},{2,6},{3,7},{4,0},{5,1},{6,2},{7,3},{8,12},{9,13},{10,... | collective-permute-start | bytes 393224 | tf_op jit(solution)/shard_map/ppermute | solution.py:251
  79.7 12.9 %collective-permute-start.14 = (bf16[128,512]{1,0:T(8,128)(2,1)S(1)}, bf16[128,512]{1,0:T(8,128)(2,1)S(1)}, u32[]{:S(2)}, u32[]{:S(2)}) collective-permute-start(bf16[128,512]{1,0:T(8,128)(2,1)S(1)} %get-tuple-element.55), channel_id=1, source_target_pairs={{0,8},{1,9},{2,10},{3,11},{4,12},{5,13},{6,14},{7,15},{8,0},{9,1},... | collective-permute-start | bytes 393224 | tf_op jit(solution)/shard_map/ppermute | solution.py:251
  81.8 11.6 %collective-permute-start.15 = (bf16[128,512]{1,0:T(8,128)(2,1)S(1)}, bf16[128,512]{1,0:T(8,128)(2,1)S(1)}, u32[]{:S(2)}, u32[]{:S(2)}) collective-permute-start(bf16[128,512]{1,0:T(8,128)(2,1)S(1)} %get-tuple-element.56), channel_id=1, source_target_pairs={{0,12},{1,13},{2,14},{3,15},{4,8},{5,9},{6,10},{7,11},{8,4},{9,5},... | collective-permute-start | bytes 393224 | tf_op jit(solution)/shard_map/ppermute | solution.py:251
  83.3 11.3 %collective-permute-start.20 = (bf16[128,512]{1,0:T(8,128)(2,1)S(1)}, bf16[128,512]{1,0:T(8,128)(2,1)S(1)}, u32[]{:S(2)}, u32[]{:S(2)}) collective-permute-start(bf16[128,512]{1,0:T(8,128)(2,1)S(1)} %get-tuple-element.60), channel_id=1, source_target_pairs={{0,4},{1,5},{2,6},{3,7},{4,0},{5,1},{6,2},{7,3},{8,12},{9,13},{10,... | collective-permute-start | bytes 393224 | tf_op jit(solution)/shard_map/ppermute | solution.py:251
  84.9 16.0 %collective-permute-start.21 = (bf16[128,512]{1,0:T(8,128)(2,1)S(1)}, bf16[128,512]{1,0:T(8,128)(2,1)S(1)}, u32[]{:S(2)}, u32[]{:S(2)}) collective-permute-start(bf16[128,512]{1,0:T(8,128)(2,1)S(1)} %get-tuple-element.61), channel_id=1, source_target_pairs={{0,8},{1,9},{2,10},{3,11},{4,12},{5,13},{6,14},{7,15},{8,0},{9,1},... | collective-permute-start | bytes 393224 | tf_op jit(solution)/shard_map/ppermute | solution.py:251
  87.5 13.4 %collective-permute-start.22 = (bf16[128,512]{1,0:T(8,128)(2,1)S(1)}, bf16[128,512]{1,0:T(8,128)(2,1)S(1)}, u32[]{:S(2)}, u32[]{:S(2)}) collective-permute-start(bf16[128,512]{1,0:T(8,128)(2,1)S(1)} %get-tuple-element.62), channel_id=1, source_target_pairs={{0,12},{1,13},{2,14},{3,15},{4,8},{5,9},{6,10},{7,11},{8,4},{9,5},... | collective-permute-start | bytes 393224 | tf_op jit(solution)/shard_map/ppermute | solution.py:251
  92.6 9.2 %collective-permute-start.28 = (bf16[64,1024]{1,0:T(8,128)(2,1)S(1)}, bf16[64,1024]{1,0:T(8,128)(2,1)S(1)}, u32[]{:S(2)}, u32[]{:S(2)}) collective-permute-start(bf16[64,1024]{1,0:T(8,128)(2,1)S(1)} %get-tuple-element.76), channel_id=1, source_target_pairs={{0,2},{1,3},{2,0},{3,1},{4,6},{5,7},{6,4},{7,5},{8,10},{9,11},{10,... | collective-permute-start | bytes 393224 | tf_op jit(solution)/shard_map/ppermute | solution.py:251
  93.3 12.9 %collective-permute-start.26 = (bf16[64,1024]{1,0:T(8,128)(2,1)S(1)}, bf16[64,1024]{1,0:T(8,128)(2,1)S(1)}, u32[]{:S(2)}, u32[]{:S(2)}) collective-permute-start(bf16[64,1024]{1,0:T(8,128)(2,1)S(1)} %get-tuple-element.71), channel_id=1, source_target_pairs={{0,2},{1,3},{2,0},{3,1},{4,6},{5,7},{6,4},{7,5},{8,10},{9,11},{10,... | collective-permute-start | bytes 393224 | tf_op jit(solution)/shard_map/ppermute | solution.py:251
  101.1 10.5 %collective-permute-start.23 = (bf16[192,512]{1,0:T(8,128)(2,1)S(1)}, bf16[192,512]{1,0:T(8,128)(2,1)S(1)}, u32[]{:S(2)}, u32[]{:S(2)}) collective-permute-start(bf16[192,512]{1,0:T(8,128)(2,1)S(1)} %get-tuple-element.66), channel_id=1, source_target_pairs={{0,2},{1,3},{2,0},{3,1},{4,6},{5,7},{6,4},{7,5},{8,10},{9,11},{10,... | collective-permute-start | bytes 589832 | tf_op jit(solution)/shard_map/ppermute | solution.py:251
  101.9 7.2 %collective-permute-start.29 = (bf16[64,512]{1,0:T(8,128)(2,1)S(1)}, bf16[64,512]{1,0:T(8,128)(2,1)S(1)}, u32[]{:S(2)}, u32[]{:S(2)}) collective-permute-start(bf16[64,512]{1,0:T(8,128)(2,1)S(1)} %get-tuple-element.79), channel_id=1, source_target_pairs={{0,8},{1,9},{2,10},{3,11},{4,12},{5,13},{6,14},{7,15},{8,0},{9,1},... | collective-permute-start | bytes 196616 | tf_op jit(solution)/shard_map/ppermute | solution.py:251
  105.5 6.1 %collective-permute-start.30 = (bf16[64,512]{1,0:T(8,128)(2,1)S(1)}, bf16[64,512]{1,0:T(8,128)(2,1)S(1)}, u32[]{:S(2)}, u32[]{:S(2)}) collective-permute-start(bf16[64,512]{1,0:T(8,128)(2,1)S(1)} %get-tuple-element.80), channel_id=1, source_target_pairs={{0,12},{1,13},{2,14},{3,15},{4,8},{5,9},{6,10},{7,11},{8,4},{9,5},... | collective-permute-start | bytes 196616 | tf_op jit(solution)/shard_map/ppermute | solution.py:251
  106.3 5.3 %collective-permute-start.27 = (bf16[64,512]{1,0:T(8,128)(2,1)S(1)}, bf16[64,512]{1,0:T(8,128)(2,1)S(1)}, u32[]{:S(2)}, u32[]{:S(2)}) collective-permute-start(bf16[64,512]{1,0:T(8,128)(2,1)S(1)} %get-tuple-element.75), channel_id=1, source_target_pairs={{0,4},{1,5},{2,6},{3,7},{4,0},{5,1},{6,2},{7,3},{8,12},{9,13},{10,... | collective-permute-start | bytes 196616 | tf_op jit(solution)/shard_map/ppermute | solution.py:251
